TPU v7x, 32 devices: a whole 2x2x4 slice. The times are simulated.
32 devices in a mesh: groups: 2 (over y), seq: 4 (over z), head: 2 (over x), sub: 2 (over core).
Axes of the slice: x: 2, y: 2, z: 4, core: 2. Of those that a mesh axis runs over, the one named last changes fastest.
Arguments:
- tokens: int32 [3, 4096], P(None, ('groups', 'seq')), parts along dimension 1, may hold values from 0 to 1023
- masked: int32 [4096], P(('groups', 'seq')), parts along dimension 0, may hold values 0 or 1
- used_frames: int32 [2], P('groups'), parts along dimension 0, may hold values from 1024 to 2048
- tables: bfloat16 [3, 1024, 1024], P(None, None, ('head', 'sub')), may hold values from -6 to 6
- mask_vec: bfloat16 [1024], P(('head', 'sub')), may hold values from -6 to 6
- attn_in: bfloat16 [3, 1024, 512], P(None, None, ('head', 'sub')), may hold values from -0.1875 to 0.1875
- head_temp: float32 [8], P(('head', 'sub')), may hold values from 12 to 28
- attn_out: bfloat16 [512, 1024], P(('head', 'sub')), may hold values from -0.25 to 0.25
- conv_in: bfloat16 [2, 1024, 1024], P(None, None, ('head', 'sub')), may hold values from -0.1875 to 0.1875
- conv_kernel: float32 [31, 1024], P(None, ('head', 'sub')), may hold values from -1 to 1
- conv_out: bfloat16 [1024, 1024], P(('head', 'sub')), may hold values from -0.1875 to 0.1875
- voc_in: bfloat16 [1024, 512], P(('head', 'sub')), may hold values from -0.1875 to 0.1875
- voc_kernel: float32 [7, 512], replicated, may hold values from -2 to 2
- voc_up: bfloat16 [512, 1536], P(('head', 'sub')), may hold values from -0.25 to 0.25
- voc_down: bfloat16 [1536, 512], P(('head', 'sub')), may hold values from -0.15625 to 0.15625
- voc_head: bfloat16 [512, 1282], P(('head', 'sub')), may hold values from -0.25 to 0.25
- head_bias: float32 [1282], replicated, may hold values from 0.5 to 2.5
Outputs:
- features: bfloat16 [4096, 1024], P(('groups', 'seq', 'head', 'sub')), parts along dimension 0
- waveform: float32 [1310720], P(('groups', 'seq', 'head', 'sub')), parts along dimension 0
There are 2 independent parts, one for each index of `groups`. A program takes and returns all parts, laid end to end along the dimension named above; an argument that names none is the same for every part. Nothing has to cross between parts.
All inputs are finite; a program needn't handle non-finite values. No bound on the sum of `masked` on one device may be relied on, other than what follows from the above.
Results may differ from a plain program's by a relative error of at most 0.02.
Values may be sent and summed in bfloat16 or wider, within the bound.
A program may use at most 64 MiB of HBM per device.

v0:
```python
import math

import jax
import jax.numpy as jnp
from jax import lax
from jax.sharding import PartitionSpec as P

HOP = 320


def with_halo(x, sides, width):
    for axis, dim in sides:
        size, length = (lax.axis_size(axis), x.shape[dim])
        up = [(i, (i + 1) % size) for i in range(size - 1)]
        down = [(j, i) for i, j in up]
        last = lax.slice_in_dim(x, length - width, length, axis=dim)
        initial = lax.slice_in_dim(x, 0, width, axis=dim)
        before = lax.ppermute(last, axis, up)
        after = lax.ppermute(initial, axis, down)
        x = jnp.concatenate([before, x, after], axis=dim)
    return x


def layer_norm(values):
    average = jnp.mean(values, axis=-1, keepdims=True)
    centered = values - average
    return centered * lax.rsqrt(jnp.mean(centered * centered, axis=-1, keepdims=True) + 1e-05)


def unit_heads(projected, head_count):
    row_count = projected.shape[0]
    split_heads = projected.reshape(row_count, head_count, projected.shape[1] // head_count)
    scaled = split_heads * lax.rsqrt(
        jnp.sum(split_heads * split_heads, axis=-1, keepdims=True) + 1e-06
    )
    return scaled.astype(jnp.bfloat16)


def depthwise(kernel, padded_rows):
    tap_count = kernel.shape[0]
    out_rows = padded_rows.shape[0] - tap_count + 1
    result = jnp.zeros((out_rows, padded_rows.shape[1]), jnp.float32)
    for offset in range(tap_count):
        result = result + kernel[offset] * padded_rows[offset : offset + out_rows].astype(
            jnp.float32
        )
    return result


def attend_block(
    paired_sums,
    key_tile_rows,
    value_tile_rows,
    leading_row,
    query_normalized,
    similarity_sharpness,
    frame_ceiling,
):
    weighted, normalizer = paired_sums
    row_count = key_tile_rows.shape[0]
    angular_similarity = jnp.einsum(
        "qhd,khd->hqk", query_normalized, key_tile_rows, preferred_element_type=jnp.float32
    )
    token_position = leading_row + lax.broadcasted_iota(jnp.int32, (1, 1, row_count), 2)
    attention_probabilities = jnp.where(
        token_position < frame_ceiling,
        jnp.exp(similarity_sharpness[:, None, None] * (angular_similarity - 1.0)),
        0.0,
    )
    normalizer = normalizer + jnp.sum(attention_probabilities, axis=2).T
    weighted = weighted + jnp.einsum(
        "hqk,khd->qhd",
        attention_probabilities.astype(jnp.bfloat16),
        value_tile_rows,
        preferred_element_type=jnp.float32,
    )
    return (weighted, normalizer)


def synthesis_tables(bin_count, fft_size):
    bin_ids = lax.broadcasted_iota(jnp.int32, (bin_count, fft_size), 0)
    sample_ids = lax.broadcasted_iota(jnp.int32, (bin_count, fft_size), 1)
    phase_angle = 2.0 * math.pi / fft_size * (bin_ids * sample_ids % fft_size).astype(jnp.float32)
    edge_bin = (bin_ids == 0) | (bin_ids == bin_count - 1)
    factor = jnp.where(edge_bin, 1.0, 2.0) / fft_size
    cos_table = factor * jnp.cos(phase_angle)
    sin_table = jnp.where(edge_bin, 0.0, -factor * jnp.sin(phase_angle))
    return jnp.concatenate([cos_table, sin_table], axis=0)


def local(
    tokens,
    masked,
    used_frames,
    tables,
    mask_vec,
    attn_in,
    head_temp,
    attn_out,
    conv_in,
    conv_kernel,
    conv_out,
    voc_in,
    voc_kernel,
    voc_up,
    voc_down,
    voc_head,
    head_bias,
):
    frame_count = tokens.shape[1]
    group_count = lax.axis_size(("head", "sub"))
    group_index = lax.axis_index(("head", "sub"))
    seq_index = lax.axis_index("seq")
    slab_rows = frame_count // group_count
    frame_ceiling = used_frames[0]
    total_frames = frame_count * lax.axis_size("seq")
    code_ids = lax.broadcasted_iota(jnp.int32, (frame_count, tables.shape[1]), 1)
    masked_rows = masked == 1
    embedded = masked_rows.astype(jnp.float32)[:, None] * mask_vec.astype(jnp.float32)[None, :]
    for rvq_level in range(3):
        matches = tokens[rvq_level][:, None] == code_ids
        if rvq_level == 2:
            matches = matches & jnp.logical_not(masked_rows)[:, None]
        embedded = embedded + jnp.dot(
            matches.astype(jnp.bfloat16), tables[rvq_level], preferred_element_type=jnp.float32
        )
    embedded = embedded.astype(jnp.bfloat16)
    inputs, voc_in_full, voc_up_full, voc_down_full, voc_head_full = (
        lax.all_gather(embedded, ("head", "sub"), axis=1, tiled=True),
        lax.all_gather(voc_in, ("head", "sub"), axis=0, tiled=True),
        lax.all_gather(voc_up, ("head", "sub"), axis=0, tiled=True),
        lax.all_gather(voc_down, ("head", "sub"), axis=0, tiled=True),
        lax.all_gather(voc_head, ("head", "sub"), axis=0, tiled=True),
    )
    normed = layer_norm(inputs.astype(jnp.float32)).astype(jnp.bfloat16)
    local_heads = head_temp.shape[0]
    query_normalized = unit_heads(
        jnp.dot(normed, attn_in[0], preferred_element_type=jnp.float32), local_heads
    )
    key_unit = unit_heads(
        jnp.dot(normed, attn_in[1], preferred_element_type=jnp.float32), local_heads
    ).reshape(frame_count, -1)
    value_rows = jnp.dot(normed, attn_in[2], preferred_element_type=jnp.float32).astype(
        jnp.bfloat16
    )
    head_size = value_rows.shape[1] // local_heads
    start_pair = (
        jnp.zeros((frame_count, local_heads, head_size), jnp.float32),
        jnp.zeros((frame_count, local_heads), jnp.float32),
    )
    paired_sums = start_pair
    key_piece = lax.all_gather(key_unit, "seq", axis=0, tiled=True)
    value_piece = lax.all_gather(value_rows, "seq", axis=0, tiled=True)
    row_count = key_piece.shape[0]
    key_heads = key_piece.reshape(row_count, local_heads, head_size)
    value_heads = value_piece.reshape(row_count, local_heads, head_size)
    block_count = row_count // 512

    def scan_step(inner_pair, block_item):
        key_tile_rows, value_tile_rows, block_index = block_item
        return (
            attend_block(
                inner_pair,
                key_tile_rows,
                value_tile_rows,
                block_index * 512,
                query_normalized,
                head_temp,
                frame_ceiling,
            ),
            None,
        )

    block_items = (
        key_heads.reshape(block_count, 512, local_heads, head_size),
        value_heads.reshape(block_count, 512, local_heads, head_size),
        jnp.arange(block_count, dtype=jnp.int32),
    )
    paired_sums, _unused = lax.scan(scan_step, paired_sums, block_items)
    weighted, normalizer = paired_sums
    attended = (weighted / normalizer[:, :, None]).reshape(frame_count, -1).astype(jnp.bfloat16)
    head_part = jnp.dot(attended, attn_out, preferred_element_type=jnp.float32)
    fft_size = 2 * (head_bias.shape[0] // 2 - 1)
    intersection = fft_size // HOP
    half_voc = voc_kernel.shape[0] // 2
    vocoder_rim = half_voc + intersection // 2
    conv_reach = conv_kernel.shape[0] // 2 + vocoder_rim
    window_rows = slab_rows + 2 * vocoder_rim
    stream = inputs.astype(jnp.float32) + lax.psum(
        head_part.astype(jnp.bfloat16), ("head", "sub")
    ).astype(jnp.float32)
    stream_rims = with_halo(stream.astype(jnp.bfloat16), (("seq", 0),), conv_reach).astype(
        stream.dtype
    )
    conv_normed = layer_norm(stream_rims).astype(jnp.bfloat16)
    residual_window = lax.dynamic_slice_in_dim(
        stream_rims, group_index * slab_rows + conv_reach - vocoder_rim, window_rows, 0
    )
    gate_value = jnp.dot(conv_normed, conv_in[0], preferred_element_type=jnp.float32)
    gate_signal = jnp.dot(conv_normed, conv_in[1], preferred_element_type=jnp.float32)
    gated_rows = (gate_value * jax.nn.sigmoid(gate_signal)).astype(jnp.bfloat16)
    depth_rows = depthwise(conv_kernel, gated_rows)
    activated = (depth_rows * jax.nn.sigmoid(depth_rows)).astype(jnp.bfloat16)
    windows = jnp.stack(
        [
            activated[member * slab_rows : member * slab_rows + window_rows]
            for member in range(group_count)
        ]
    )
    partial_out = jnp.einsum("gsc,cd->gsd", windows, conv_out, preferred_element_type=jnp.float32)
    conv_sum = lax.psum_scatter(
        partial_out.astype(jnp.bfloat16), ("head", "sub"), scatter_dimension=0, tiled=True
    ).astype(jnp.float32)[0]
    block_norm = layer_norm(residual_window + conv_sum).astype(jnp.bfloat16)
    feature_out = block_norm[vocoder_rim : vocoder_rim + slab_rows]
    first_frame = seq_index * frame_count + group_index * slab_rows - vocoder_rim
    frame_ids = first_frame + lax.broadcasted_iota(jnp.int32, (window_rows, 1), 0)
    live_rows = (frame_ids >= 0) & (frame_ids < frame_ceiling)
    base_rows = layer_norm(
        jnp.where(
            live_rows, jnp.dot(block_norm, voc_in_full, preferred_element_type=jnp.float32), 0.0
        )
    )
    vdepth = depthwise(voc_kernel, base_rows)
    voc_rows = vdepth.shape[0]
    inner_rows = layer_norm(vdepth).astype(jnp.bfloat16)
    hidden = jax.nn.gelu(
        jnp.dot(inner_rows, voc_up_full, preferred_element_type=jnp.float32), approximate=False
    ).astype(jnp.bfloat16)
    refined = base_rows[half_voc : half_voc + voc_rows] + jnp.dot(
        hidden, voc_down_full, preferred_element_type=jnp.float32
    )
    head_input = layer_norm(refined).astype(jnp.bfloat16)
    spectrum = jnp.dot(head_input, voc_head_full, preferred_element_type=jnp.float32) + head_bias
    bin_count = spectrum.shape[1] // 2
    magnitude = jnp.minimum(jnp.exp(spectrum[:, :bin_count]), 100.0)
    phase_rows = spectrum[:, bin_count:]
    coefficients = jnp.concatenate(
        [magnitude * jnp.cos(phase_rows), magnitude * jnp.sin(phase_rows)], axis=1
    )
    wave_rows = jnp.dot(
        coefficients, synthesis_tables(bin_count, fft_size), precision=lax.Precision.HIGHEST
    )
    sample_ids = lax.broadcasted_iota(jnp.int32, (fft_size,), 0).astype(jnp.float32)
    hann_window = 0.5 - 0.5 * jnp.cos(2.0 * math.pi / fft_size * sample_ids)
    wave_ids = first_frame + half_voc + lax.broadcasted_iota(jnp.int32, (voc_rows, 1), 0)
    exists = ((wave_ids >= 0) & (wave_ids < total_frames)).astype(jnp.float32)
    framed = (wave_rows * hann_window[None, :] * exists).reshape(voc_rows, intersection, HOP)
    env_rows = (exists * (hann_window * hann_window)[None, :]).reshape(voc_rows, intersection, HOP)
    audio_sum = jnp.zeros((slab_rows, HOP), jnp.float32)
    energy = jnp.zeros((slab_rows, HOP), jnp.float32)
    for quarter in range(intersection):
        begin = intersection - quarter
        audio_sum = audio_sum + framed[begin : begin + slab_rows, quarter]
        energy = energy + env_rows[begin : begin + slab_rows, quarter]
    waveform = (audio_sum / energy).reshape(slab_rows * HOP)
    return (feature_out, waveform)


def solution(mesh):
    in_specs = (
        P(None, ("groups", "seq")),
        P(("groups", "seq")),
        P("groups"),
        P(None, None, ("head", "sub")),
        P(("head", "sub")),
        P(None, None, ("head", "sub")),
        P(("head", "sub")),
        P(("head", "sub"), None),
        P(None, None, ("head", "sub")),
        P(None, ("head", "sub")),
        P(("head", "sub"), None),
        P(("head", "sub"), None),
        P(),
        P(("head", "sub"), None),
        P(("head", "sub"), None),
        P(("head", "sub"), None),
        P(),
    )
    out_specs = (P(("groups", "seq", "head", "sub"), None), P(("groups", "seq", "head", "sub")))
    return jax.shard_map(local, mesh=mesh, in_specs=in_specs, out_specs=out_specs, check_vma=False)
```

profile of v0, /device:TPU:0, one launch (start us, length us, event | category | flops | bytes accessed | tf_op | source)
XLA Modules:
  0.0 276.2 jit_solution(7080855097597714248)
XLA Ops:
  9.4 1.6 fusion.39
  11.0 1.6 fusion.38
  12.6 2.3 fusion.41
  16.1 18.6 %all-gather.6.cloned.1.call-done = bf16[512,1024]{1,0:T(8,128)(2,1)} async-done(((bf16[512,256]{1,0:T(8,128)(2,1)}), bf16[512,1024]{1,0:T(8,128)(2,1)}) %all-gather.6.cloned.1.call-update) | async-done | bytes 1048592 | tf_op jit(solution)/shard_map/all_gather | solution.py:129
  36.2 1.6 fusion.24
  40.1 16.0 %all_gather.23 = bf16[2048,128]{0,1:T(8,128)(2,1)S(1)} all-gather(bf16[512,128]{0,1:T(8,128)(2,1)S(1)} %bitcast.157), channel_id=1, replica_groups=mesh['groups'=2,'seq'=4,'head'=2,'sub'=2] {'seq'}, dimensions={0}, use_global_device_ids=true | all-gather | bytes 655360 | tf_op jit(solution)/shard_map/all_gather | solution.py:152
  57.3 1.9 copy.28
  59.2 2.1 multiply_reduce_fusion.5
  61.4 16.1 %all_gather.22 = bf16[2048,128]{1,0:T(8,128)(2,1)S(1)} all-gather(bf16[512,128]{1,0:T(8,128)(2,1)S(1)} %convolution_convert_fusion.2), channel_id=1, replica_groups=mesh['groups'=2,'seq'=4,'head'=2,'sub'=2] {'seq'}, dimensions={0}, use_global_device_ids=true | all-gather | bytes 655360 | tf_op jit(solution)/shard_map/all_gather | solution.py:153
  79.6 15.6 %while.15 = (s32[]{:T(128)}, f32[512,2,64]{0,2,1:T(8,128)S(1)}, f32[512,2]{0,1:T(2,128)S(1)}, bf16[4,512,2,64]{1,3,2,0:T(8,128)(2,1)S(1)}, s32[4]{0:T(128)S(1)},...) while((s32[]{:T(128)}, f32[512,2,64]{0,2,1:T(8,128)S(1)}, ...), condition=%wide.region_6.7_spmd.clone, body=%wide.region_4.6_spmd.clone.sunk | while | flops 136972288 | bytes 3032748 | solution.py:179
  81.5 1.6 bitcast_reduce_fusion.2
  85.5 1.6 bitcast_reduce_fusion.2
  89.4 1.6 bitcast_reduce_fusion.2
  93.3 1.6 bitcast_reduce_fusion.2
  95.3 2.4 convolution_convert_fusion.1
  97.9 36.0 %all-reduce.2.cloned.1.call-done = bf16[512,1024]{1,0:T(8,128)(2,1)} async-done(((bf16[512,1024]{1,0:T(8,128)(2,1)}), bf16[512,1024]{1,0:T(8,128)(2,1)}) %all-reduce.2.cloned.1.call-update) | async-done | bytes 1048592 | tf_op jit(solution)/shard_map/psum | solution.py:189
  133.9 1.7 fusion.26
  135.6 3.4 %collective-permute-start = (bf16[20,1024]{1,0:T(8,128)(2,1)S(1)}, bf16[20,1024]{1,0:T(8,128)(2,1)S(1)}, u32[]{:S(2)}, u32[]{:S(2)}) collective-permute-start(bf16[20,1024]{1,0:T(8,128)(2,1)S(1)} %get-tuple-element.190), channel_id=1, source_target_pairs={{0,4},{4,8},{8,12},{1,5},{5,9},{9,13},{2,6},{6,10},{10,14},{3,7},{... | collective-permute-start | bytes 122888 | tf_op jit(solution)/shard_map/ppermute | solution.py:18
  140.8 4.3 %collective-permute-done.1 = bf16[20,1024]{1,0:T(8,128)(2,1)S(1)} collective-permute-done((bf16[20,1024]{1,0:T(8,128)(2,1)S(1)}, bf16[20,1024]{1,0:T(8,128)(2,1)S(1)}, u32[]{:S(2)}, u32[]{:S(2)}) %collective-permute-start.1) | collective-permute-done | bytes 40992 | tf_op jit(solution)/shard_map/ppermute | solution.py:19
  147.6 2.3 multiply_convert_fusion.2
  155.0 15.1 %multiply_select_fusion = (f32[641,1280]{1,0:T(8,128)}, f32[641,1280]{1,0:T(8,128)}) fusion(f32[641]{0:T(1024)S(1)} %fusion.133, pred[641]{0:T(1024)(128)(4,1)S(1)} %fusion.132, f32[641]{0:T(1024)S(1)} %select_multiply_fusion), kind=kLoop, calls=%fused_computation.20 | loop fusion | flops 9845760 | bytes 6569609 | tf_op jit(solution)/shard_map/jit(_where)/select_n | solution.py:87
  170.1 1.8 fusion.166
  171.9 4.9 %reduce-scatter.2.cloned.1.call-done = bf16[1,138,1024]{2,1,0:T(8,128)(2,1)} async-done(((bf16[4,138,1024]{2,1,0:T(8,128)(2,1)}), bf16[1,138,1024]{2,1,0:T(8,128)(2,1)}) %reduce-scatter.2.cloned.1.call-update) | async-done | bytes 282640 | tf_op jit(solution)/shard_map/reduce_scatter | solution.py:211
  180.9 14.1 %all-gather.8.cloned.1.call-done = bf16[1024,512]{1,0:T(8,128)(2,1)} async-done(((bf16[256,512]{1,0:T(8,128)(2,1)}), bf16[1024,512]{1,0:T(8,128)(2,1)}) %all-gather.8.cloned.1.call-update) | async-done | bytes 1048592 | tf_op jit(solution)/shard_map/all_gather | solution.py:130
  194.9 1.7 fusion.177
  198.3 17.7 %all-gather.10.cloned.1.call-done = bf16[512,1536]{1,0:T(8,128)(2,1)} async-done(((bf16[128,1536]{1,0:T(8,128)(2,1)}), bf16[512,1536]{1,0:T(8,128)(2,1)}) %all-gather.10.cloned.1.call-update) | async-done | bytes 1572880 | tf_op jit(solution)/shard_map/all_gather | solution.py:131
  216.0 21.1 %all-gather.12.cloned.1.call-done = bf16[1536,512]{1,0:T(8,128)(2,1)} async-done(((bf16[384,512]{1,0:T(8,128)(2,1)}), bf16[1536,512]{1,0:T(8,128)(2,1)}) %all-gather.12.cloned.1.call-update) | async-done | bytes 1572880 | tf_op jit(solution)/shard_map/all_gather | solution.py:132
  237.1 4.3 %fusion.178 = (f32[132]{0:T(256)S(1)}, f32[132,512]{1,0:T(8,128)S(1)}) fusion(bf16[1536,512]{1,0:T(8,128)(2,1)} %all-gather.12.cloned.1.call-done, bf16[512,1536]{1,0:T(8,128)(2,1)} %all-gather.10.cloned.1.call-done, f32[132,512]{1,0:T(8,128)S(1)} %get-tuple-element.185, f32[132]{0:T(256)S(1)} %add_rsqrt_fusion.5, f32[132]{0:T(256)S(1)} %broadcast_multiply_fusion.4, ...), kind=kOutput, calls=%fused_computation.260 | convolution fusion | flops 428752768 | bytes 3958320 | tf_op jit(solution)/shard_map/dot_general | solution.py:230
  241.6 15.4 %all-gather.14.cloned.1.call-done = bf16[512,1282]{0,1:T(8,128)(2,1)} async-done(((bf16[128,1282]{0,1:T(8,128)(2,1)}), bf16[512,1282]{0,1:T(8,128)(2,1)}) %all-gather.14.cloned.1.call-update) | async-done | bytes 1312784 | tf_op jit(solution)/shard_map/all_gather | solution.py:133
  257.0 2.1 convolution_add_fusion
  259.2 1.9 cosine_multiply_fusion.1
  261.1 6.2 %fusion.19 = f32[132,1280]{1,0:T(8,128)S(1)} fusion(f32[641,1280]{1,0:T(8,128)S(1)} %copy-done.2, f32[641,1280]{1,0:T(8,128)} %get-tuple-element.254, f32[132,641]{1,0:T(8,128)S(1)} %get-tuple-element.199, f32[132,641]{1,0:T(8,128)S(1)} %get-tuple-element.198, f32[132]{0:T(256)S(1)} %and_convert_fusion, f32[1280]{0:T(1024)S(1)} %multiply_subtract_fusion), kind=kOutput, calls=%fused_computation.31 | convolution fusion | flops 2601428736 | bytes 7922224 | tf_op jit(solution)/shard_map/dot_general | solution.py:241
  (115 shorter events, 33.3 us)
Async XLA Ops:
  7.2 142.8 %copy-start = (bf16[256,1024]{1,0:T(8,128)(2,1)S(1)}, bf16[256,1024]{1,0:T(8,128)(2,1)}, u32[]{:S(2)}) copy-start(bf16[256,1024]{1,0:T(8,128)(2,1)} %param.29) | copy-start | bytes 1572868
  7.2 27.5 %all-gather.6.cloned.1.call-start = ((), (), s32[]{:S(2)}) async-start(), calls=%async_computation.1 | async-start | bytes 1310720 | tf_op jit(solution)/shard_map/all_gather | solution.py:129
  11.0 4.1 %copy-start.3 = (bf16[3,1024,128]{2,1,0:T(8,128)(2,1)S(1)}, bf16[3,1024,128]{2,1,0:T(8,128)(2,1)}, u32[]{:S(2)}) copy-start(bf16[3,1024,128]{2,1,0:T(8,128)(2,1)} %param.24) | copy-start | bytes 2359300
  14.9 119.0 %all-reduce.2.cloned.1.call-start = ((), (), s32[]{:S(2)}) async-start(), calls=%async_computation.2 | async-start | bytes 2097152 | tf_op jit(solution)/shard_map/psum | solution.py:189
  34.6 3.2 %copy-start.1 = (bf16[512,1024]{1,0:T(8,128)(2,1)S(1)}, bf16[512,1024]{1,0:T(8,128)(2,1)}, u32[]{:S(2)}) copy-start(bf16[512,1024]{1,0:T(8,128)(2,1)} %all-gather.6.cloned.1.call-done) | copy-start | bytes 3145732
  61.4 18.3 %copy-start.8 = (f32[2]{0:T(128)S(1)}, f32[2]{0:T(128)}, u32[]{:S(2)}) copy-start(f32[2]{0:T(128)} %param.25) | copy-start | bytes 28
  95.3 2.6 copy-start.4
  97.8 79.0 %reduce-scatter.2.cloned.1.call-start = ((), (), s32[]{:S(2)}) async-start(), calls=%async_computation.3 | async-start | bytes 1474560 | tf_op jit(solution)/shard_map/reduce_scatter | solution.py:211
  133.9 12.1 %copy-start.7 = (bf16[2,1024,256]{2,1,0:T(8,128)(2,1)S(1)}, bf16[2,1024,256]{2,1,0:T(8,128)(2,1)}, u32[]{:S(2)}) copy-start(bf16[2,1024,256]{2,1,0:T(8,128)(2,1)} %param.27) | copy-start | bytes 3145732
  135.6 5.1 %collective-permute-start = (bf16[20,1024]{1,0:T(8,128)(2,1)S(1)}, bf16[20,1024]{1,0:T(8,128)(2,1)S(1)}, u32[]{:S(2)}, u32[]{:S(2)}) collective-permute-start(bf16[20,1024]{1,0:T(8,128)(2,1)S(1)} %get-tuple-element.190), channel_id=1, source_target_pairs={{0,4},{4,8},{8,12},{1,5},{5,9},{9,13},{2,6},{6,10},{10,14},{3,7},{... | collective-permute-start | bytes 122888 | tf_op jit(solution)/shard_map/ppermute | solution.py:18
  139.0 6.0 %collective-permute-start.1 = (bf16[20,1024]{1,0:T(8,128)(2,1)S(1)}, bf16[20,1024]{1,0:T(8,128)(2,1)S(1)}, u32[]{:S(2)}, u32[]{:S(2)}) collective-permute-start(bf16[20,1024]{1,0:T(8,128)(2,1)S(1)} %get-tuple-element.191), channel_id=1, source_target_pairs={{4,0},{8,4},{12,8},{5,1},{9,5},{13,9},{6,2},{10,6},{14,10},{7,3},{... | collective-permute-start | bytes 122888 | tf_op jit(solution)/shard_map/ppermute | solution.py:19
  149.9 4.8 %copy-start.5 = (f32[7,512]{1,0:T(8,128)S(1)}, f32[7,512]{1,0:T(8,128)}, u32[]{:S(2)}) copy-start(f32[7,512]{1,0:T(8,128)} %param.31) | copy-start | bytes 43012
  151.5 43.5 %all-gather.8.cloned.1.call-start = ((), (), s32[]{:S(2)}) async-start(), calls=%async_computation.4 | async-start | bytes 1310720 | tf_op jit(solution)/shard_map/all_gather | solution.py:130
  152.0 64.0 %all-gather.10.cloned.1.call-start = ((), (), s32[]{:S(2)}) async-start(), calls=%async_computation.5 | async-start | bytes 1966080 | tf_op jit(solution)/shard_map/all_gather | solution.py:131
  152.6 84.5 %all-gather.12.cloned.1.call-start = ((), (), s32[]{:S(2)}) async-start(), calls=%async_computation.6 | async-start | bytes 1966080 | tf_op jit(solution)/shard_map/all_gather | solution.py:132
  153.2 103.8 %all-gather.14.cloned.1.call-start = ((), (), s32[]{:S(2)}) async-start(), calls=%async_computation.7 | async-start | bytes 1648640 | tf_op jit(solution)/shard_map/all_gather | solution.py:133
  198.3 58.8 %copy-start.6 = (f32[1282]{0:T(1024)S(1)}, f32[1282]{0:T(1024)}, u32[]{:S(2)}) copy-start(f32[1282]{0:T(1024)} %param.35) | copy-start | bytes 15388
  257.0 4.0 %copy-start.2 = (f32[641,1280]{1,0:T(8,128)S(1)}, f32[641,1280]{1,0:T(8,128)}, u32[]{:S(2)}) copy-start(f32[641,1280]{1,0:T(8,128)} %get-tuple-element.253) | copy-start | bytes 9845764
Sparse Core Ops, SparseCore 0:
  15.1 19.5 all-gather.5
  97.9 35.9 all-reduce.1
  151.6 25.1 reduce-scatter.1
  178.2 16.6 all-gather.7
  196.3 19.6 all-gather.9
  217.4 19.6 all-gather.11
  238.6 18.3 all-gather.13
where the time goes:
time: 277 us; the launch traced here: 276 us
  waiting for transfers between devices  135 us (49%)
  other arithmetic  38 us (14%)
  matrix products  37 us (13%)
  blocking collectives  32.1 us (12%)
  between operations  15.2 us (5%)
  local copies, waits for them, and re-layouts  11.3 us (4%)
  starting transfers between devices  5.14 us (2%)
  loops' own time  2.77 us (1%)
    psum x1, waiting for transfers between devices, local(): lax.psum(head_part.astype(jnp.bfloat16), ('head', 'sub'))  36 us
    all_gather x1, waiting for transfers between devices, local(): lax.all_gather(voc_down, ('head', 'sub'), axis=0, tiled=True)  21.1 us
    all_gather x1, waiting for transfers between devices, local(): lax.all_gather(embedded, ('head', 'sub'), axis=1, tiled=True)  18.6 us
    all_gather x1, waiting for transfers between devices, local(): lax.all_gather(voc_up, ('head', 'sub'), axis=0, tiled=True)  17.7 us
    all_gather x1, blocking collectives, local(): value_piece = lax.all_gather(value_rows, 'seq', axis=0, tiled=True)  16.1 us
    all_gather x1, blocking collectives, local(): key_piece = lax.all_gather(key_unit, 'seq', axis=0, tiled=True)  16 us
    all_gather x1, waiting for transfers between devices, local(): lax.all_gather(voc_head, ('head', 'sub'), axis=0, tiled=True)  15.4 us
    select_n x1, other arithmetic, synthesis_tables(): sin_table = jnp.where(edge_bin, 0.0, -factor * jnp.sin(phase_angle))  15.1 us
  transfers between devices with their start and end apart: 9, of which 9 were waited for; matrix products, arithmetic and copies ran while one was open for 11% of the time, Pallas kernels for 0%

commit v1 on v0

v1 whole, which is shorter than its diff:
```python
import functools
import math

import jax
import jax.numpy as jnp
from jax import lax
from jax.experimental import pallas as pl
from jax.experimental.pallas import tpu as pltpu
from jax.sharding import PartitionSpec as P

HOP = 320


def layer_norm(values):
    average = jnp.mean(values, axis=-1, keepdims=True)
    centered = values - average
    return centered * lax.rsqrt(jnp.mean(centered * centered, axis=-1, keepdims=True) + 1e-05)


def depthwise(kernel, padded_rows):
    tap_count = kernel.shape[0]
    out_rows = padded_rows.shape[0] - tap_count + 1
    result = jnp.zeros((out_rows, padded_rows.shape[1]), jnp.float32)
    for offset in range(tap_count):
        result = result + kernel[offset] * padded_rows[offset : offset + out_rows].astype(
            jnp.float32
        )
    return result


def synthesis_tables(bin_count, fft_size, window):
    fine = 16
    coarse = -(-bin_count // fine)
    unit = 2.0 * math.pi / fft_size
    samples = lax.broadcasted_iota(jnp.int32, (coarse, fft_size), 1)
    steps = lax.broadcasted_iota(jnp.int32, (coarse, fft_size), 0) * fine
    big = unit * (steps * samples % fft_size).astype(jnp.float32)
    samples = lax.broadcasted_iota(jnp.int32, (fine, fft_size), 1)
    steps = lax.broadcasted_iota(jnp.int32, (fine, fft_size), 0)
    small = unit * (steps * samples % fft_size).astype(jnp.float32)
    big_cos, big_sin, small_cos, small_sin = lax.optimization_barrier(
        (jnp.cos(big) * window, jnp.sin(big) * window, jnp.cos(small), jnp.sin(small))
    )
    cosine = big_cos[:, None] * small_cos[None] - big_sin[:, None] * small_sin[None]
    sine = big_sin[:, None] * small_cos[None] + big_cos[:, None] * small_sin[None]
    bins = lax.broadcasted_iota(jnp.int32, (coarse * fine, 1), 0)
    edge = (bins == 0) | (bins == bin_count - 1)
    factor = jnp.where(edge, 1.0, 2.0) / fft_size
    cosine = factor * cosine.reshape(coarse * fine, fft_size)
    sine = jnp.where(edge, 0.0, -factor * sine.reshape(coarse * fine, fft_size))
    return cosine[:bin_count].astype(jnp.bfloat16), sine[:bin_count].astype(jnp.bfloat16)


MESH = pl.DeviceIdType.MESH
HALO = 32


def remote(src, dst, send_sem, recv_sem, **where):
    return pltpu.make_async_remote_copy(
        src_ref=src,
        dst_ref=dst,
        send_sem=send_sem,
        recv_sem=recv_sem,
        device_id=where,
        device_id_type=MESH,
    )


class Place:
    def __init__(self):
        self.group, self.seq = lax.axis_index("groups"), lax.axis_index("seq")
        self.head, self.sub = lax.axis_index("head"), lax.axis_index("sub")
        self.groups, self.seqs = lax.axis_size("groups"), lax.axis_size("seq")
        self.heads = lax.axis_size("head")
        self.me = self.head * 2 + self.sub
        self.partner = 1 - self.sub

    def head_at(self, step):
        return lax.rem(self.head + step, self.heads)

    def group_at(self, step):
        return lax.rem(self.group + step, self.groups)


def enter(at, with_seq):
    barrier = pltpu.get_barrier_semaphore()
    for step in range(1, at.heads):
        pl.semaphore_signal(barrier, inc=1, device_id={"head": at.head_at(step)}, device_id_type=MESH)
    for step in range(1, at.groups):
        pl.semaphore_signal(barrier, inc=1, device_id={"groups": at.group_at(step)}, device_id_type=MESH)
    pl.semaphore_signal(barrier, inc=1, device_id={"sub": at.partner}, device_id_type=MESH)
    count = at.heads + at.groups - 1
    if with_seq:

        @pl.when(at.seq > 0)
        def _():
            pl.semaphore_signal(barrier, inc=1, device_id={"seq": at.seq - 1}, device_id_type=MESH)

        @pl.when(at.seq < at.seqs - 1)
        def _():
            pl.semaphore_signal(barrier, inc=1, device_id={"seq": at.seq + 1}, device_id_type=MESH)

        count = (
            count
            + jnp.where(at.seq > 0, 1, 0)
            + jnp.where(at.seq < at.seqs - 1, 1, 0)
        )
    pl.semaphore_wait(barrier, count)


class Spread:
    def __init__(self, at, buffer, rows, sems):
        self.at, self.buffer, self.rows = at, buffer, rows
        self.send, self.recv = sems

    def part(self, block):
        return self.buffer.at[block, pl.ds(*self.rows)]

    def cross(self, step):
        block = self.part(self.at.me)
        return remote(
            block, block, self.send.at[step], self.recv.at[step], head=self.at.head_at(step)
        )

    def aside(self, step):
        block = self.part(self.at.head_at(self.at.heads - step) * 2 + self.at.sub)
        slot = self.at.heads + step
        return remote(block, block, self.send.at[slot], self.recv.at[slot], sub=self.at.partner)

    def start(self):
        for step in range(1, self.at.heads):
            self.cross(step).start()
        self.aside(0).start()

    def relay(self):
        for step in range(1, self.at.heads):
            self.cross(step).wait_recv()
            self.aside(step).start()

    def finish(self):
        for step in range(self.at.heads):
            if step > 0:
                self.cross(step).wait_send()
            self.aside(step).wait()


class Weight:
    def __init__(self, at, own, full, sems):
        self.at, self.own, self.full = at, own, full
        self.send, self.recv, self.local = sems
        self.length = own.shape[0] // at.groups

    def piece(self, block, part):
        start = pl.multiple_of(part * self.length, 16)
        return self.full.at[block, pl.ds(start, self.length)]

    def source(self, step):
        return self.at.head_at(self.at.heads - step) * 2 + self.at.sub

    def cross(self, step):
        start = pl.multiple_of(self.at.group * self.length, 16)
        return remote(
            self.own.at[pl.ds(start, self.length)],
            self.piece(self.at.me, self.at.group),
            self.send.at[step],
            self.recv.at[step],
            head=self.at.head_at(step),
        )

    def over(self, step, turn):
        block = self.piece(self.source(step), self.at.group)
        slot = self.at.heads + (step - 1) * self.at.groups + turn
        return remote(
            block, block, self.send.at[slot], self.recv.at[slot], groups=self.at.group_at(turn)
        )

    def aside(self, step, turn):
        part = self.at.group_at(self.at.groups - turn)
        block = self.piece(self.source(step), part)
        slot = self.at.heads * (1 + self.at.groups) + (step - 1) * self.at.groups + turn
        return remote(block, block, self.send.at[slot], self.recv.at[slot], sub=self.at.partner)

    def mine(self):
        return remote(
            self.own, self.full.at[self.at.me], self.send.at[0], self.recv.at[0], sub=self.at.partner
        )

    def kept(self):
        return pltpu.make_async_copy(self.own, self.full.at[self.at.me], self.local.at[0])

    def start(self):
        for step in range(1, self.at.heads):
            self.cross(step).start()
        self.mine().start()
        self.kept().start()

    def relay_cross(self):
        for step in range(1, self.at.heads):
            self.cross(step).wait_recv()
            for turn in range(1, self.at.groups):
                self.over(step, turn).start()
            self.aside(step, 0).start()

    def relay_over(self):
        for step in range(1, self.at.heads):
            for turn in range(1, self.at.groups):
                self.over(step, turn).wait_recv()
                self.aside(step, turn).start()

    def finish(self):
        self.mine().wait()
        self.kept().wait()
        for step in range(1, self.at.heads):
            self.cross(step).wait_send()
            for turn in range(1, self.at.groups):
                self.over(step, turn).wait_send()
            for turn in range(self.at.groups):
                self.aside(step, turn).wait()


def weight_sems(heads, groups):
    count = heads * (1 + 2 * groups)
    return [
        pltpu.SemaphoreType.DMA((count,)),
        pltpu.SemaphoreType.DMA((count,)),
        pltpu.SemaphoreType.DMA((1,)),
    ]


def norm_rows(values):
    average = jnp.mean(values, axis=-1, keepdims=True)
    centered = values - average
    return centered * lax.rsqrt(jnp.mean(centered * centered, axis=-1, keepdims=True) + 1e-05)


def attention_kernel(weight_count, head_size, *refs):
    used_ref, temp_ref, tok_ref, tables_ref, mask_ref, attn_ref = refs[:6]
    owns = refs[6 : 6 + weight_count]
    refs = refs[6 + weight_count :]
    emb_out, att_out = refs[:2]
    fulls = refs[2 : 2 + weight_count]
    refs = refs[2 + weight_count :]
    (tokh, emb, att, kvbuf, q_scr, acc, l_acc, tok_send, tok_recv, e_send, e_recv, a_send, a_recv,
     r_send, r_recv, l_send, l_recv) = refs[:17]
    wsems = refs[17:]
    at = Place()
    rows = tok_ref.shape[0]
    total = rows + 2 * HALO
    blocks = emb.shape[0]
    codes = tables_ref.shape[1]
    local_heads = q_scr.shape[0]
    width = q_scr.shape[2]
    tokh[...] = jnp.zeros_like(tokh)
    enter(at, True)
    first, last = at.seq == 0, at.seq == at.seqs - 1

    def tokens_up():
        return remote(tok_ref.at[pl.ds(rows - HALO, HALO)], tokh.at[pl.ds(0, HALO)],
                      tok_send.at[0], tok_recv.at[0], seq=at.seq + 1)

    def tokens_down():
        return remote(tok_ref.at[pl.ds(0, HALO)], tokh.at[pl.ds(HALO, HALO)],
                      tok_send.at[1], tok_recv.at[1], seq=at.seq - 1)

    @pl.when(jnp.logical_not(last))
    def _():
        tokens_up().start()

    @pl.when(jnp.logical_not(first))
    def _():
        tokens_down().start()

    weights = [
        Weight(at, owns[w], fulls[w], wsems[3 * w : 3 * w + 3]) for w in range(weight_count)
    ]

    def embed(token_rows):
        count = token_rows.shape[0]
        ids = lax.broadcasted_iota(jnp.int32, (count, codes), 1)
        result = token_rows[:, 3:4].astype(jnp.float32) * mask_ref[...].astype(jnp.float32)
        for level in range(3):
            hot = jnp.where(token_rows[:, level : level + 1] == ids, 1.0, 0.0).astype(jnp.bfloat16)
            result = result + jnp.dot(hot, tables_ref[level], preferred_element_type=jnp.float32)
        return result.astype(jnp.bfloat16)

    half = rows // 2
    cut = half // 2
    spreads = [
        Spread(at, emb, (0, half), (e_send.at[0], e_recv.at[0])),
        Spread(at, emb, (half, total - half), (e_send.at[1], e_recv.at[1])),
    ]
    for chunk in range(2):
        emb[at.me, pl.ds(chunk * cut, cut)] = embed(tok_ref[pl.ds(chunk * cut, cut)])
    spreads[0].start()
    for chunk in range(2, 4):
        emb[at.me, pl.ds(chunk * cut, cut)] = embed(tok_ref[pl.ds(chunk * cut, cut)])

    @pl.when(jnp.logical_not(last))
    def _():
        tokens_up().wait_send()

    @pl.when(jnp.logical_not(first))
    def _():
        tokens_up().wait_recv()
        tokens_down().wait_send()

    @pl.when(jnp.logical_not(last))
    def _():
        tokens_down().wait_recv()

    emb[at.me, pl.ds(rows, 2 * HALO)] = embed(tokh[...])
    spreads[1].start()
    for weight in weights:
        weight.start()

    lanes = lax.broadcasted_iota(jnp.int32, (1, width), 1)
    in_head = [
        (lanes >= h * head_size) & (lanes < (h + 1) * head_size) for h in range(local_heads)
    ]

    def unit(projected):
        squares = projected * projected
        scale = jnp.zeros_like(projected)
        for h in range(local_heads):
            total_h = jnp.sum(jnp.where(in_head[h], squares, 0.0), axis=-1, keepdims=True)
            scale = jnp.where(in_head[h], lax.rsqrt(total_h + 1e-06), scale)
        return projected * scale

    own_kv = kvbuf.at[at.seq]
    step_rows = 64
    for index, spread in enumerate(spreads):
        spread.relay()
        spread.finish()
        begin, count = spread.rows
        piece = count // 2 if count // 2 % 32 == 0 else count
        for offset in range(begin, begin + count, piece):
            size = piece
            whole = jnp.concatenate(
                [emb[block, pl.ds(offset, size)] for block in range(blocks)], axis=1
            )
            emb_out[pl.ds(offset, size)] = whole
            normed = norm_rows(whole.astype(jnp.float32)).astype(jnp.bfloat16)
            query = unit(jnp.dot(normed, attn_ref[0], preferred_element_type=jnp.float32))
            for h in range(local_heads):
                q_scr[h, pl.ds(offset, size)] = jnp.where(in_head[h], query, 0.0).astype(jnp.bfloat16)
            kept = min(size, rows - offset)
            if kept > 0:
                normed = normed[:kept]
                own_kv[0, pl.ds(offset, kept)] = unit(
                    jnp.dot(normed, attn_ref[1], preferred_element_type=jnp.float32)
                ).astype(jnp.bfloat16)
                own_kv[1, pl.ds(offset, kept)] = jnp.dot(
                    normed, attn_ref[2], preferred_element_type=jnp.float32
                ).astype(jnp.bfloat16)

    def send_up(block, step):
        view = kvbuf.at[block]
        return remote(view, view, r_send.at[step], r_recv.at[step], seq=at.seq + 1)

    def send_down(block, step):
        view = kvbuf.at[block]
        return remote(view, view, l_send.at[step], l_recv.at[step], seq=at.seq - 1)

    @pl.when(jnp.logical_not(last))
    def _():
        send_up(at.seq, 0).start()

    @pl.when(jnp.logical_not(first))
    def _():
        send_down(at.seq, 0).start()

    acc[...] = jnp.zeros_like(acc)
    l_acc[...] = jnp.zeros_like(l_acc)
    tile = total // 3

    def attend(block):
        frame = block * rows + lax.broadcasted_iota(jnp.int32, (1, rows), 1)
        live = frame < used_ref[0]
        for h in range(local_heads):
            sharp = temp_ref[h] * 1.4426950408889634
            bias = jnp.where(live, -sharp, -1e30)

            def one(index, carry):
                span = pl.ds(pl.multiple_of(index * tile, 64), tile)
                scores = lax.dot_general(
                    q_scr[h, span],
                    kvbuf[block, 0],
                    (((1,), (1,)), ((), ())),
                    preferred_element_type=jnp.float32,
                )
                chance = jnp.exp2(scores * sharp + bias)
                part = chance[:, :128]
                for lane in range(128, rows, 128):
                    part = part + chance[:, lane : lane + 128]
                l_acc[h, span] += part
                acc[h, span] += jnp.dot(
                    chance.astype(jnp.bfloat16), kvbuf[block, 1], preferred_element_type=jnp.float32
                )
                return carry

            lax.fori_loop(0, 3, one, 0)

    def exchange(step):
        @pl.when(step < at.seq)
        def _():
            block = at.seq - 1 - step
            send_up(block, step).wait_recv()

            @pl.when(jnp.logical_not(last))
            def _():
                send_up(block, step + 1).start()

            attend(block)

        @pl.when(step < at.seqs - 1 - at.seq)
        def _():
            block = at.seq + 1 + step
            send_down(block, step).wait_recv()

            @pl.when(jnp.logical_not(first))
            def _():
                send_down(block, step + 1).start()

            attend(block)

    attend(at.seq)
    weights[0].relay_cross()
    if at.seqs > 1:
        exchange(0)
    weights[0].relay_over()
    for weight in weights[1:2]:
        weight.relay_cross()

    def later(step, carry):
        exchange(step)
        return carry

    lax.fori_loop(1, at.seqs - 1, later, 0)
    value = jnp.zeros((total, width), jnp.float32)
    for h in range(local_heads):
        mean = acc[h] / jnp.sum(l_acc[h], axis=-1, keepdims=True)
        value = jnp.where(in_head[h], mean, value)
    att[at.me] = value.astype(jnp.bfloat16)
    gather = Spread(at, att, (0, total), (a_send, a_recv))
    gather.start()
    for weight in weights[2:]:
        weight.relay_cross()
    for weight in weights[1:]:
        weight.relay_over()
    gather.relay()

    def drain(step, carry):
        @pl.when(jnp.logical_not(last) & (step <= at.seq))
        def _():
            send_up(at.seq - step, step).wait_send()

        @pl.when(jnp.logical_not(first) & (step <= at.seqs - 1 - at.seq))
        def _():
            send_down(at.seq + step, step).wait_send()

        return carry

    lax.fori_loop(0, at.seqs - 1, drain, 0)
    gather.finish()
    for block in range(blocks):
        att_out[block] = att[block]
    for weight in weights:
        weight.finish()


def attention(used_frames, head_temp, packed, tables, mask_vec, attn_in, owns, blocks):
    groups, heads, seqs = (lax.axis_size(name) for name in ("groups", "head", "seq"))
    rows = packed.shape[0]
    total = rows + 2 * HALO
    width = attn_in.shape[2]
    local_heads = head_temp.shape[0]
    columns = tables.shape[2]
    vmem = pl.BlockSpec(memory_space=pltpu.VMEM)
    smem = pl.BlockSpec(memory_space=pltpu.SMEM)
    dma = pltpu.SemaphoreType.DMA
    sems = []
    for _ in owns:
        sems += weight_sems(heads, groups)
    return pl.pallas_call(
        functools.partial(attention_kernel, len(owns), width // local_heads),
        out_shape=[
            jax.ShapeDtypeStruct((total, columns * blocks), jnp.bfloat16),
            jax.ShapeDtypeStruct((blocks, total, width), jnp.bfloat16),
        ]
        + [jax.ShapeDtypeStruct((blocks,) + own.shape, own.dtype) for own in owns],
        in_specs=[smem, smem] + [vmem] * (4 + len(owns)),
        out_specs=[vmem, vmem] + [pl.BlockSpec(memory_space=pl.ANY)] * len(owns),
        scratch_shapes=[
            pltpu.VMEM((2 * HALO, packed.shape[1]), jnp.int32),
            pltpu.VMEM((blocks, total, columns), jnp.bfloat16),
            pltpu.VMEM((blocks, total, width), jnp.bfloat16),
            pltpu.VMEM((seqs, 2, rows, width), jnp.bfloat16),
            pltpu.VMEM((local_heads, total, width), jnp.bfloat16),
            pltpu.VMEM((local_heads, total, width), jnp.float32),
            pltpu.VMEM((local_heads, total, 128), jnp.float32),
            dma((2,)),
            dma((2,)),
            dma((2, 2 * heads)),
            dma((2, 2 * heads)),
            dma((2 * heads,)),
            dma((2 * heads,)),
            dma((seqs,)),
            dma((seqs,)),
            dma((seqs,)),
            dma((seqs,)),
        ]
        + sems,
        compiler_params=pltpu.CompilerParams(collective_id=0, has_side_effects=True, vmem_limit_bytes=60 * 1024 * 1024),
    )(used_frames, head_temp, packed, tables, mask_vec.reshape(1, -1), attn_in, *owns)


def swap_kernel(weight_count, *refs):
    win_ref = refs[0]
    owns = refs[1 : 1 + weight_count]
    out_ref = refs[1 + weight_count]
    fulls = refs[2 + weight_count : 2 + 2 * weight_count]
    act, send, recv = refs[2 + 2 * weight_count : 5 + 2 * weight_count]
    wsems = refs[5 + 2 * weight_count :]
    at = Place()
    blocks = at.heads * 2
    barrier = pltpu.get_barrier_semaphore()
    peers = []
    for step in range(at.heads):
        for other in range(2):
            if step or other:
                peers.append((step, other))
    for step, other in peers:
        pl.semaphore_signal(
            barrier,
            inc=1,
            device_id={"head": at.head_at(step), "sub": lax.rem(at.sub + other, 2)},
            device_id_type=MESH,
        )
    for step in range(1, at.groups):
        pl.semaphore_signal(barrier, inc=1, device_id={"groups": at.group_at(step)}, device_id_type=MESH)
    pl.semaphore_wait(barrier, blocks - 1 + at.groups - 1)
    copies = []
    for slot, (step, other) in enumerate(peers):
        head, sub = at.head_at(step), lax.rem(at.sub + other, 2)
        copies.append(
            remote(win_ref.at[head * 2 + sub], act.at[at.me], send.at[slot], recv.at[slot], head=head, sub=sub)
        )
        copies[-1].start()
    weights = [
        Weight(at, owns[w], fulls[w], wsems[3 * w : 3 * w + 3]) for w in range(weight_count)
    ]
    for weight in weights:
        weight.start()
    act[at.me] = win_ref[at.me]
    for weight in weights:
        weight.relay_cross()
    for weight in weights:
        weight.relay_over()
    for slot, (step, other) in enumerate(peers):
        copies[slot].wait_send()
        source = at.head_at(at.heads - step) * 2 + lax.rem(at.sub + other, 2)
        remote(win_ref.at[source], act.at[source], send.at[slot], recv.at[slot],
               head=at.head_at(step), sub=lax.rem(at.sub + other, 2)).wait_recv()
    out_ref[...] = act[...]
    for weight in weights:
        weight.finish()


def swap(windows, owns):
    groups, heads = lax.axis_size("groups"), lax.axis_size("head")
    vmem = pl.BlockSpec(memory_space=pltpu.VMEM)
    dma = pltpu.SemaphoreType.DMA
    sems = []
    for _ in owns:
        sems += weight_sems(heads, groups)
    blocks = windows.shape[0]
    return pl.pallas_call(
        functools.partial(swap_kernel, len(owns)),
        out_shape=[jax.ShapeDtypeStruct(windows.shape, windows.dtype)]
        + [jax.ShapeDtypeStruct((blocks,) + own.shape, own.dtype) for own in owns],
        in_specs=[vmem] * (1 + len(owns)),
        out_specs=[vmem] + [pl.BlockSpec(memory_space=pl.ANY)] * len(owns),
        scratch_shapes=[
            pltpu.VMEM(windows.shape, windows.dtype),
            dma((blocks,)),
            dma((blocks,)),
        ]
        + sems,
        compiler_params=pltpu.CompilerParams(collective_id=1, has_side_effects=True),
    )(windows, *owns)


def local(
    tokens,
    masked,
    used_frames,
    tables,
    mask_vec,
    attn_in,
    head_temp,
    attn_out,
    conv_in,
    conv_kernel,
    conv_out,
    voc_in,
    voc_kernel,
    voc_up,
    voc_down,
    voc_head,
    head_bias,
):
    frame_count = tokens.shape[1]
    group_count = lax.axis_size(("head", "sub"))
    group_index = lax.axis_index(("head", "sub"))
    seq_index = lax.axis_index("seq")
    slab_rows = frame_count // group_count
    frame_ceiling = used_frames[0]
    total_frames = frame_count * lax.axis_size("seq")
    masked_rows = masked == 1
    packed = jnp.stack(
        [
            tokens[0],
            tokens[1],
            jnp.where(masked_rows, -1, tokens[2]),
            masked_rows.astype(jnp.int32),
        ],
        axis=1,
    )
    packed = jnp.pad(packed, ((0, 0), (0, 124)))
    embedded, attended, attn_out_full, conv_out_full, voc_in_flat3 = attention(
        used_frames, head_temp, packed, tables, mask_vec, attn_in, (attn_out, conv_out, voc_in), group_count
    )
    fft_size = 2 * (head_bias.shape[0] // 2 - 1)
    intersection = fft_size // HOP
    half_voc = voc_kernel.shape[0] // 2
    vocoder_rim = half_voc + intersection // 2
    conv_reach = conv_kernel.shape[0] // 2 + vocoder_rim
    window_rows = slab_rows + 2 * vocoder_rim
    stream_rows = embedded.astype(jnp.float32) + jnp.einsum(
        "grc,gcd->rd", attended, attn_out_full, preferred_element_type=jnp.float32
    )
    stream_rims = jnp.concatenate(
        [
            stream_rows[frame_count + HALO - conv_reach : frame_count + HALO],
            stream_rows[:frame_count],
            stream_rows[frame_count + HALO : frame_count + HALO + conv_reach],
        ]
    )
    rim_ids = seq_index * frame_count - conv_reach + lax.broadcasted_iota(
        jnp.int32, (frame_count + 2 * conv_reach, 1), 0
    )
    stream_rims = jnp.where((rim_ids >= 0) & (rim_ids < total_frames), stream_rims, 0.0)
    conv_normed = layer_norm(stream_rims).astype(jnp.bfloat16)
    residual_window = lax.dynamic_slice_in_dim(
        stream_rims, group_index * slab_rows + conv_reach - vocoder_rim, window_rows, 0
    )
    gate_value = jnp.dot(conv_normed, conv_in[0], preferred_element_type=jnp.float32)
    gate_signal = jnp.dot(conv_normed, conv_in[1], preferred_element_type=jnp.float32)
    gated_rows = (gate_value * jax.nn.sigmoid(gate_signal)).astype(jnp.bfloat16)
    depth_rows = depthwise(conv_kernel, gated_rows)
    activated = (depth_rows * jax.nn.sigmoid(depth_rows)).astype(jnp.bfloat16)
    windows = jnp.stack(
        [
            activated[member * slab_rows : member * slab_rows + window_rows]
            for member in range(group_count)
        ]
    )
    pad_rows = -window_rows % 16
    windows = jnp.pad(windows, ((0, 0), (0, pad_rows), (0, 0)))
    swapped, voc_up_flat3, voc_down_flat3, voc_head_flat3 = swap(windows, (voc_up, voc_down, voc_head))
    voc_in_flat, voc_up_flat, voc_down_flat, voc_head_flat = (
        full.reshape(-1, full.shape[2])
        for full in (voc_in_flat3, voc_up_flat3, voc_down_flat3, voc_head_flat3)
    )
    conv_sum = jnp.einsum(
        "gsc,gcd->sd", swapped[:, :window_rows], conv_out_full, preferred_element_type=jnp.float32
    )
    block_norm = layer_norm(residual_window + conv_sum).astype(jnp.bfloat16)
    feature_out = block_norm[vocoder_rim : vocoder_rim + slab_rows]
    first_frame = seq_index * frame_count + group_index * slab_rows - vocoder_rim
    frame_ids = first_frame + lax.broadcasted_iota(jnp.int32, (window_rows, 1), 0)
    live_rows = (frame_ids >= 0) & (frame_ids < frame_ceiling)
    base_rows = layer_norm(
        jnp.where(
            live_rows, jnp.dot(block_norm, voc_in_flat, preferred_element_type=jnp.float32), 0.0
        )
    )
    vdepth = depthwise(voc_kernel, base_rows)
    voc_rows = vdepth.shape[0]
    inner_rows = layer_norm(vdepth).astype(jnp.bfloat16)
    hidden = jax.nn.gelu(
        jnp.dot(inner_rows, voc_up_flat, preferred_element_type=jnp.float32), approximate=False
    ).astype(jnp.bfloat16)
    refined = base_rows[half_voc : half_voc + voc_rows] + jnp.dot(
        hidden, voc_down_flat, preferred_element_type=jnp.float32
    )
    head_input = layer_norm(refined).astype(jnp.bfloat16)
    spectrum = jnp.dot(head_input, voc_head_flat, preferred_element_type=jnp.float32) + head_bias
    bin_count = spectrum.shape[1] // 2
    magnitude = jnp.minimum(jnp.exp(spectrum[:, :bin_count]), 100.0)
    phase_rows = spectrum[:, bin_count:]
    coefficients = jnp.concatenate(
        [magnitude * jnp.cos(phase_rows), magnitude * jnp.sin(phase_rows)], axis=1
    )
    sample_ids = lax.broadcasted_iota(jnp.int32, (fft_size,), 0).astype(jnp.float32)
    hann_window = 0.5 - 0.5 * jnp.cos(2.0 * math.pi / fft_size * sample_ids)
    cosine_table, sine_table = synthesis_tables(bin_count, fft_size, hann_window)
    wave_rows = jnp.dot(
        (magnitude * jnp.cos(phase_rows)).astype(jnp.bfloat16), cosine_table, preferred_element_type=jnp.float32
    ) + jnp.dot(
        (magnitude * jnp.sin(phase_rows)).astype(jnp.bfloat16), sine_table, preferred_element_type=jnp.float32
    )
    wave_ids = first_frame + half_voc + lax.broadcasted_iota(jnp.int32, (voc_rows, 1), 0)
    exists = ((wave_ids >= 0) & (wave_ids < total_frames)).astype(jnp.float32)
    framed = (wave_rows * exists).reshape(voc_rows, intersection, HOP)
    env_rows = (exists * (hann_window * hann_window)[None, :]).reshape(voc_rows, intersection, HOP)
    audio_sum = jnp.zeros((slab_rows, HOP), jnp.float32)
    energy = jnp.zeros((slab_rows, HOP), jnp.float32)
    for quarter in range(intersection):
        begin = intersection - quarter
        audio_sum = audio_sum + framed[begin : begin + slab_rows, quarter]
        energy = energy + env_rows[begin : begin + slab_rows, quarter]
    waveform = (audio_sum / energy).reshape(slab_rows * HOP)
    return (feature_out, waveform)


def solution(mesh):
    in_specs = (
        P(None, ("groups", "seq")),
        P(("groups", "seq")),
        P("groups"),
        P(None, None, ("head", "sub")),
        P(("head", "sub")),
        P(None, None, ("head", "sub")),
        P(("head", "sub")),
        P(("head", "sub"), None),
        P(None, None, ("head", "sub")),
        P(None, ("head", "sub")),
        P(("head", "sub"), None),
        P(("head", "sub"), None),
        P(),
        P(("head", "sub"), None),
        P(("head", "sub"), None),
        P(("head", "sub"), None),
        P(),
    )
    out_specs = (P(("groups", "seq", "head", "sub"), None), P(("groups", "seq", "head", "sub")))
    return jax.shard_map(local, mesh=mesh, in_specs=in_specs, out_specs=out_specs, check_vma=False)
```

time: 277 us -> 123 us (0.44)
  waiting for transfers between devices: 135 us -> 0 us
  Pallas kernels: 0 us -> 81.2 us
  blocking collectives: 32.1 us -> 0 us
  other arithmetic: 38 us -> 10.7 us
  matrix products: 37 us -> 18.4 us
  between operations: 15.2 us -> 1.65 us
  starting transfers between devices: 5.14 us -> 0 us
  loops' own time: 2.77 us -> 0 us
    all_gather x5 -> x0, waiting for transfers between devices: 86.9 us -> none  [the longest x1 21.1 us: local(): lax.all_gather(voc_down, ('head', 'sub'), axis=0, tiled=True)]
    pallas_call x0 -> x2, Pallas kernels: none -> 81.2 us  [the longest x1 53.2 us: attention(): pl.pallas_call(functools.partial(attention_kernel, len(owns), width // lo...]
    psum x1 -> x0, waiting for transfers between devices: 36 us -> none  [local(): lax.psum(head_part.astype(jnp.bfloat16), ('head', 'sub'))]
    all_gather x2 -> x0, blocking collectives: 32.1 us -> none  [the longest x1 16.1 us: local(): value_piece = lax.all_gather(value_rows, 'seq', axis=0, tiled=True)]
    dot_general x20 -> x7, matrix products: 35.5 us -> 17.4 us  [the longest x1 4.39 us: local(): jnp.dot(hidden, voc_down_flat, preferred_element_type=jnp.float32)]
    select_n x1, other arithmetic: 15.1 us -> 0.69 us  [local(): jnp.where(masked_rows, -1, tokens[2])]
    convert_element_type x8 -> x1, other arithmetic: 5.47 us -> 0.28 us  [local(): conv_normed = layer_norm(stream_rims).astype(jnp.bfloat16)]
    reduce_scatter x1 -> x0, waiting for transfers between devices: 4.9 us -> none  [local(): lax.psum_scatter(partial_out.astype(jnp.bfloat16), ('head', 'sub'), scatt...]
  transfers between devices with their start and end apart: 9 -> 0, of which waited for: 9 -> 0; matrix products, arithmetic and copies ran while one was open for 11% -> 0% of each run, Pallas kernels for 0% -> 0%
where the time goes in v1:
time: 123 us; the launch traced here: 122 us
  Pallas kernels  81.2 us (66%)
  matrix products  18.4 us (15%)
  other arithmetic  10.7 us (9%)
  local copies, waits for them, and re-layouts  10.3 us (8%)
  between operations  1.65 us (1%)
    pallas_call x1, Pallas kernels, attention(): pl.pallas_call(functools.partial(attention_kernel, len(owns), width // lo...  53.2 us
    pallas_call x1, Pallas kernels, swap(): pl.pallas_call(functools.partial(swap_kernel, len(owns)), out_shape=[jax....  28 us
    dot_general x1, matrix products, local(): jnp.dot(hidden, voc_down_flat, preferred_element_type=jnp.float32)  4.39 us
    dot_general x1, matrix products, local(): jnp.dot((magnitude * jnp.sin(phase_rows)).astype(jnp.bfloat16), sine_tabl...  4.32 us
    dot_general x1, matrix products, local(): jnp.dot((magnitude * jnp.cos(phase_rows)).astype(jnp.bfloat16), cosine_ta...  2.87 us
    dot_general x1, matrix products, local(): jnp.einsum('grc,gcd->rd', attended, attn_out_full, preferred_element_type...  2.54 us
    convert_element_type x1, other arithmetic, local(): activated = (depth_rows * jax.nn.sigmoid(depth_rows)).astype(jnp.bfloat16)  2.52 us

profile of v1, /device:TPU:0, one launch (start us, length us, event | category | flops | bytes accessed | tf_op | source)
XLA Modules:
  0.0 122.3 jit_solution(2075239657771058467)
XLA Ops:
  0.6 0.8 slice_bitcast_fusion.5
  1.4 0.7 broadcast_select_fusion
  2.3 0.7 pad.8.refs_2_
  3.7 1.2 reshape.195.refs_4_
  4.9 53.2 %shard_map.176 = (bf16[576,1024]{1,0:T(8,128)(2,1)}, bf16[4,576,128]{2,1,0:T(8,128)(2,1)}, bf16[4,128,1024]{2,1,0:T(8,128)(2,1)}, bf16[4,256,1024]{2,1,0:T(8,128)(2,1)}, bf16[4,256,512]{2,1,0:T(8,128)(2,1)}) custom-call(s32[1]{0:T(128)} %copy.49.refs_0_, f32[2]{0:T(128)} %refs_1_.2, s32[512,128]{1,0:T(8,128)} %pad.8.refs_2_, bf16[3,1024,256]{2,1,0:T(8,128)(2,1)} %refs_3_.2, ...), custom_call_target="tpu_custom_call" | custom-call | tf_op jit(solution)/shard_map/pallas_call | solution.py:484
  58.1 2.5 %bitcast_add_fusion = f32[576,1024]{1,0:T(8,128)S(1)} fusion(bf16[576,1024]{1,0:T(8,128)(2,1)} %get-tuple-element.15, bf16[4,576,128]{2,1,0:T(8,128)(2,1)} %get-tuple-element.16, bf16[4,128,1024]{2,1,0:T(8,128)(2,1)} %get-tuple-element.17), kind=kOutput, calls=%fused_computation.10 | convolution fusion | flops 605159424 | bytes 5177344 | tf_op jit(solution)/shard_map/grc,gcd->rd/dot_general | solution.py:639
  60.7 1.4 %slice.412 = f32[512,1024]{1,0:T(8,128)} slice(f32[576,1024]{1,0:T(8,128)S(1)} %bitcast_add_fusion), slice={[0:512], [0:1024]} | slice | bytes 4194304 | tf_op jit(solution)/shard_map/slice | solution.py:645
  62.1 2.0 %fusion.140 = (f32[552]{0:T(1024)S(1)}, f32[552,1024]{1,0:T(8,128)S(1)}) fusion(f32[20,1024]{1,0:T(8,128)S(1)} %get-tuple-element.35, f32[512,1024]{1,0:T(8,128)} %slice.412, f32[20,1024]{1,0:T(8,128)S(1)} %get-tuple-element.34, pred[552]{0:T(1024)(128)(4,1)S(1)} %fusion.102), kind=kLoop, calls=%fused_computation.217 | loop fusion | flops 2260440 | bytes 4524744 | tf_op jit(solution)/shard_map/reduce_sum | solution.py:15
  64.2 0.4 multiply_reduce_fusion
  64.6 0.3 multiply_convert_fusion
  64.9 0.9 copy-done.9
  65.8 0.5 fusion.32
  66.3 0.5 fusion.16
  66.8 0.2 copy-done.6
  67.1 2.5 %multiply_convert_fusion.2 = bf16[522,256]{1,0:T(8,128)(2,1)S(1)} fusion(bf16[552,256]{1,0:T(8,128)(2,1)S(1)} %fusion.16, f32[256]{0:T(256)S(1)} %bitcast.133, f32[256]{0:T(256)S(1)} %bitcast.134, f32[256]{0:T(256)S(1)} %bitcast.105, f32[256]{0:T(256)S(1)} %bitcast.106, f32[256]{0:T(256)S(1)} %bitcast.107, f32[256]{0:T(256)S(1)} %bitcast.108, ...), kind=kLoop, calls=%fused_computation.55 | loop fusion | flops 12962304 | bytes 8584192 | tf_op jit(solution)/shard_map/convert_element_type | solution.py:661
  69.6 0.8 fusion.70.refs_0_
  70.4 0.9 copy.30.refs_3_
  71.3 28.0 %shard_map.177 = (bf16[4,144,256]{2,1,0:T(8,128)(2,1)}, bf16[4,128,1536]{2,1,0:T(8,128)(2,1)}, bf16[4,384,512]{2,1,0:T(8,128)(2,1)}, bf16[4,128,1282]{2,1,0:T(8,128)(2,1)}) custom-call(bf16[4,144,256]{2,1,0:T(8,128)(2,1)} %fusion.70.refs_0_, bf16[128,1536]{1,0:T(8,128)(2,1)} %refs_1_.3, bf16[384,512]{1,0:T(8,128)(2,1)} %refs_2_.1, ...), custom_call_target="tpu_custom_call" | custom-call | tf_op jit(solution)/shard_map/pallas_call | solution.py:577
  99.3 2.4 %fusion.146 = (f32[138]{0:T(256)S(1)}, f32[138,1024]{1,0:T(8,128)S(1)}) fusion(bf16[4,256,1024]{2,1,0:T(8,128)(2,1)} %get-tuple-element.19, bf16[4,144,256]{2,1,0:T(8,128)(2,1)} %get-tuple-element.18, f32[552,1024]{1,0:T(8,128)S(1)} %get-tuple-element.31, s32[]{:T(128)S(6)} %select_n.52), kind=kOutput, calls=%fused_computation.223 | convolution fusion | flops 289689472 | bytes 3523116 | tf_op jit(solution)/shard_map/gsc,gcd->sd/dot_general | solution.py:675
  102.1 0.4 fusion.147
  103.0 0.3 fusion.138
  103.5 4.4 %fusion.148 = (f32[132]{0:T(256)S(1)}, f32[132,512]{1,0:T(8,128)S(1)}) fusion(bf16[1536,512]{1,0:T(8,128)(2,1)} %bitcast.137, bf16[512,1536]{1,0:T(8,128)(2,1)} %bitcast.136, f32[132,512]{1,0:T(8,128)S(1)} %get-tuple-element.29, f32[132]{0:T(256)S(1)} %add_rsqrt_fusion.2, f32[132]{0:T(256)S(1)} %broadcast_multiply_fusion.3, ...), kind=kOutput, calls=%fused_computation.225 | convolution fusion | flops 428752768 | bytes 3958320 | tf_op jit(solution)/shard_map/dot_general | solution.py:694
  108.2 0.4 convolution_add_fusion.1
  108.7 1.1 sine_multiply_fusion
  109.8 0.3 fusion.97
  110.1 0.7 multiply_add_fusion
  110.9 2.9 %fusion.4 = f32[132,1280]{1,0:T(8,128)} fusion(f32[656,1280]{1,0:T(8,128)S(1)} %bitcast.88, f32[641]{0:T(1024)S(1)} %bitcast.92, f32[132,1282]{1,0:T(8,128)S(1)} %convolution_add_fusion.1), kind=kOutput, calls=%fused_computation.14 | convolution fusion | flops 218501520 | bytes 4833280 | tf_op jit(solution)/shard_map/dot_general | solution.py:708
  113.8 4.3 %fusion.3 = f32[132,1280]{1,0:T(8,128)} fusion(f32[132,1280]{1,0:T(8,128)} %fusion.4, f32[656,1280]{1,0:T(8,128)S(1)} %bitcast.89, f32[641]{0:T(1024)S(1)} %bitcast.93, pred[641]{0:T(1024)(128)(4,1)S(1)} %bitcast.135, f32[132]{0:T(256)S(1)} %and_convert_fusion, f32[132,1282]{1,0:T(8,128)} %copy-done), kind=kOutput, calls=%fused_computation.8 | convolution fusion | flops 219659920 | bytes 5531648 | tf_op jit(solution)/shard_map/dot_general | solution.py:710
  118.1 1.7 %reshape.200 = f32[132,4,320]{2,1,0:T(4,128)S(1)} reshape(f32[132,1280]{1,0:T(8,128)} %fusion.3) | data formatting | bytes 1351680 | tf_op jit(solution)/shard_map/reshape | solution.py:715
  119.8 0.6 fusion.142
  120.7 0.8 div.66
  121.5 0.8 slice.449
  (53 shorter events, 1.9 us)
Async XLA Ops:
  64.5 1.2 %copy-start.9 = (bf16[2,1024,256]{2,1,0:T(8,128)(2,1)S(1)}, bf16[2,1024,256]{2,1,0:T(8,128)(2,1)}, u32[]{:S(2)}) copy-start(bf16[2,1024,256]{2,1,0:T(8,128)(2,1)} %param.25) | copy-start | bytes 3145732
  66.3 0.8 copy-start.6
  67.1 3.3 %copy-start.5 = (bf16[128,1282]{0,1:T(8,128)(2,1)S(1)}, bf16[128,1282]{0,1:T(8,128)(2,1)}, u32[]{:S(2)}) copy-start(bf16[128,1282]{0,1:T(8,128)(2,1)} %param.32) | copy-start | bytes 984580
  99.3 2.8 %copy-start.4 = (bf16[4,256,512]{2,1,0:T(8,128)(2,1)S(1)}, bf16[4,256,512]{2,1,0:T(8,128)(2,1)}, u32[]{:S(2)}) copy-start(bf16[4,256,512]{2,1,0:T(8,128)(2,1)} %get-tuple-element.20) | copy-start | bytes 3145732
  101.7 1.2 %copy-start.7 = (f32[7,512]{1,0:T(8,128)S(1)}, f32[7,512]{1,0:T(8,128)}, u32[]{:S(2)}) copy-start(f32[7,512]{1,0:T(8,128)} %param.29) | copy-start | bytes 43012
  102.1 0.7 copy-start.1
  103.5 4.6 %copy-start.3 = (bf16[4,128,1282]{2,1,0:T(8,128)(2,1)S(1)}, bf16[4,128,1282]{2,1,0:T(8,128)(2,1)}, u32[]{:S(2)}) copy-start(bf16[4,128,1282]{2,1,0:T(8,128)(2,1)} %get-tuple-element.23) | copy-start | bytes 3938308
  103.5 4.6 %copy-start.8 = (f32[1282]{0:T(1024)S(1)}, f32[1282]{0:T(1024)}, u32[]{:S(2)}) copy-start(f32[1282]{0:T(1024)} %param.33) | copy-start | bytes 15388
  108.6 2.3 %copy-start = (f32[132,1282]{1,0:T(8,128)}, f32[132,1282]{1,0:T(8,128)S(1)}, u32[]{:S(2)}) copy-start(f32[132,1282]{1,0:T(8,128)S(1)} %convolution_add_fusion.1) | copy-start | bytes 2030692
  119.8 1.7 %copy-start.2 = (bf16[138,1024]{1,0:T(8,128)(2,1)S(1)}, bf16[138,1024]{1,0:T(8,128)(2,1)}, u32[]{:S(2)}) copy-start(bf16[138,1024]{1,0:T(8,128)(2,1)} %copy-done.1) | copy-start | bytes 847876

commit v2 on v1

--- a/solution.py
+++ b/solution.py
@@ -326,8 +326,15 @@
             scale = jnp.where(in_head[h], lax.rsqrt(total_h + 1e-06), scale)
         return projected * scale
 
+    def send_up(block, step, piece):
+        view = kvbuf.at[block, piece]
+        return remote(view, view, r_send.at[step, piece], r_recv.at[step, piece], seq=at.seq + 1)
+
+    def send_down(block, step, piece):
+        view = kvbuf.at[block, piece]
+        return remote(view, view, l_send.at[step, piece], l_recv.at[step, piece], seq=at.seq - 1)
+
     own_kv = kvbuf.at[at.seq]
-    step_rows = 64
     for index, spread in enumerate(spreads):
         spread.relay()
         spread.finish()
@@ -346,35 +353,27 @@
             kept = min(size, rows - offset)
             if kept > 0:
                 normed = normed[:kept]
-                own_kv[0, pl.ds(offset, kept)] = unit(
+                own_kv[index, 0, pl.ds(offset - begin, kept)] = unit(
                     jnp.dot(normed, attn_ref[1], preferred_element_type=jnp.float32)
                 ).astype(jnp.bfloat16)
-                own_kv[1, pl.ds(offset, kept)] = jnp.dot(
+                own_kv[index, 1, pl.ds(offset - begin, kept)] = jnp.dot(
                     normed, attn_ref[2], preferred_element_type=jnp.float32
                 ).astype(jnp.bfloat16)
 
-    def send_up(block, step):
-        view = kvbuf.at[block]
-        return remote(view, view, r_send.at[step], r_recv.at[step], seq=at.seq + 1)
-
-    def send_down(block, step):
-        view = kvbuf.at[block]
-        return remote(view, view, l_send.at[step], l_recv.at[step], seq=at.seq - 1)
-
-    @pl.when(jnp.logical_not(last))
-    def _():
-        send_up(at.seq, 0).start()
-
-    @pl.when(jnp.logical_not(first))
-    def _():
-        send_down(at.seq, 0).start()
+        @pl.when(jnp.logical_not(last))
+        def _():
+            send_up(at.seq, 0, index).start()
+
+        @pl.when(jnp.logical_not(first))
+        def _():
+            send_down(at.seq, 0, index).start()
 
     acc[...] = jnp.zeros_like(acc)
     l_acc[...] = jnp.zeros_like(l_acc)
     tile = total // 3
 
-    def attend(block):
-        frame = block * rows + lax.broadcasted_iota(jnp.int32, (1, rows), 1)
+    def attend(block, piece):
+        frame = block * rows + piece * half + lax.broadcasted_iota(jnp.int32, (1, half), 1)
         live = frame < used_ref[0]
         for h in range(local_heads):
             sharp = temp_ref[h] * 1.4426950408889634
@@ -384,58 +383,63 @@
                 span = pl.ds(pl.multiple_of(index * tile, 64), tile)
                 scores = lax.dot_general(
                     q_scr[h, span],
-                    kvbuf[block, 0],
+                    kvbuf[block, piece, 0],
                     (((1,), (1,)), ((), ())),
                     preferred_element_type=jnp.float32,
                 )
                 chance = jnp.exp2(scores * sharp + bias)
                 part = chance[:, :128]
-                for lane in range(128, rows, 128):
+                for lane in range(128, half, 128):
                     part = part + chance[:, lane : lane + 128]
                 l_acc[h, span] += part
                 acc[h, span] += jnp.dot(
-                    chance.astype(jnp.bfloat16), kvbuf[block, 1], preferred_element_type=jnp.float32
+                    chance.astype(jnp.bfloat16), kvbuf[block, piece, 1], preferred_element_type=jnp.float32
                 )
                 return carry
 
             lax.fori_loop(0, 3, one, 0)
 
     def exchange(step):
-        @pl.when(step < at.seq)
-        def _():
-            block = at.seq - 1 - step
-            send_up(block, step).wait_recv()
-
-            @pl.when(jnp.logical_not(last))
+        for piece in range(2):
+
+            @pl.when(step < at.seq)
             def _():
-                send_up(block, step + 1).start()
-
-            attend(block)
-
-        @pl.when(step < at.seqs - 1 - at.seq)
-        def _():
-            block = at.seq + 1 + step
-            send_down(block, step).wait_recv()
-
-            @pl.when(jnp.logical_not(first))
+                block = at.seq - 1 - step
+                send_up(block, step, piece).wait_recv()
+
+                @pl.when(jnp.logical_not(last))
+                def _():
+                    send_up(block, step + 1, piece).start()
+
+                attend(block, piece)
+
+            @pl.when(step < at.seqs - 1 - at.seq)
             def _():
-                send_down(block, step + 1).start()
-
-            attend(block)
-
-    attend(at.seq)
-    weights[0].relay_cross()
-    if at.seqs > 1:
-        exchange(0)
-    weights[0].relay_over()
-    for weight in weights[1:2]:
-        weight.relay_cross()
+                block = at.seq + 1 + step
+                send_down(block, step, piece).wait_recv()
+
+                @pl.when(jnp.logical_not(first))
+                def _():
+                    send_down(block, step + 1, piece).start()
+
+                attend(block, piece)
 
     def later(step, carry):
         exchange(step)
         return carry
 
-    lax.fori_loop(1, at.seqs - 1, later, 0)
+    attend(at.seq, 0)
+    attend(at.seq, 1)
+    weights[0].relay_cross()
+    exchange(0)
+    weights[0].relay_over()
+    weights[1].relay_cross()
+    exchange(1)
+    for weight in weights[2:4]:
+        weight.relay_cross()
+    for weight in weights[1:3]:
+        weight.relay_over()
+    lax.fori_loop(2, at.seqs - 1, later, 0)
     value = jnp.zeros((total, width), jnp.float32)
     for h in range(local_heads):
         mean = acc[h] / jnp.sum(l_acc[h], axis=-1, keepdims=True)
@@ -443,20 +447,24 @@
     att[at.me] = value.astype(jnp.bfloat16)
     gather = Spread(at, att, (0, total), (a_send, a_recv))
     gather.start()
-    for weight in weights[2:]:
+    for weight in weights[4:]:
         weight.relay_cross()
-    for weight in weights[1:]:
+    for weight in weights[3:4]:
         weight.relay_over()
     gather.relay()
+    for weight in weights[4:]:
+        weight.relay_over()
 
     def drain(step, carry):
         @pl.when(jnp.logical_not(last) & (step <= at.seq))
         def _():
-            send_up(at.seq - step, step).wait_send()
+            for piece in range(2):
+                send_up(at.seq - step, step, piece).wait_send()
 
         @pl.when(jnp.logical_not(first) & (step <= at.seqs - 1 - at.seq))
         def _():
-            send_down(at.seq + step, step).wait_send()
+            for piece in range(2):
+                send_down(at.seq + step, step, piece).wait_send()
 
         return carry
 
@@ -494,7 +502,7 @@
             pltpu.VMEM((2 * HALO, packed.shape[1]), jnp.int32),
             pltpu.VMEM((blocks, total, columns), jnp.bfloat16),
             pltpu.VMEM((blocks, total, width), jnp.bfloat16),
-            pltpu.VMEM((seqs, 2, rows, width), jnp.bfloat16),
+            pltpu.VMEM((seqs, 2, 2, rows // 2, width), jnp.bfloat16),
             pltpu.VMEM((local_heads, total, width), jnp.bfloat16),
             pltpu.VMEM((local_heads, total, width), jnp.float32),
             pltpu.VMEM((local_heads, total, 128), jnp.float32),
@@ -504,10 +512,10 @@
             dma((2, 2 * heads)),
             dma((2 * heads,)),
             dma((2 * heads,)),
-            dma((seqs,)),
-            dma((seqs,)),
-            dma((seqs,)),
-            dma((seqs,)),
+            dma((seqs, 2)),
+            dma((seqs, 2)),
+            dma((seqs, 2)),
+            dma((seqs, 2)),
         ]
         + sems,
         compiler_params=pltpu.CompilerParams(collective_id=0, has_side_effects=True, vmem_limit_bytes=60 * 1024 * 1024),
@@ -627,9 +635,10 @@
         axis=1,
     )
     packed = jnp.pad(packed, ((0, 0), (0, 124)))
-    embedded, attended, attn_out_full, conv_out_full, voc_in_flat3 = attention(
-        used_frames, head_temp, packed, tables, mask_vec, attn_in, (attn_out, conv_out, voc_in), group_count
-    )
+    embedded, attended, *fulls = attention(
+        used_frames, head_temp, packed, tables, mask_vec, attn_in, (attn_out, conv_out, voc_in, voc_up, voc_down, voc_head), group_count
+    )
+    attn_out_full, conv_out_full = fulls[:2]
     fft_size = 2 * (head_bias.shape[0] // 2 - 1)
     intersection = fft_size // HOP
     half_voc = voc_kernel.shape[0] // 2
@@ -667,10 +676,10 @@
     )
     pad_rows = -window_rows % 16
     windows = jnp.pad(windows, ((0, 0), (0, pad_rows), (0, 0)))
-    swapped, voc_up_flat3, voc_down_flat3, voc_head_flat3 = swap(windows, (voc_up, voc_down, voc_head))
+    (swapped,) = swap(windows, ())
     voc_in_flat, voc_up_flat, voc_down_flat, voc_head_flat = (
         full.reshape(-1, full.shape[2])
-        for full in (voc_in_flat3, voc_up_flat3, voc_down_flat3, voc_head_flat3)
+        for full in fulls[2:]
     )
     conv_sum = jnp.einsum(
         "gsc,gcd->sd", swapped[:, :window_rows], conv_out_full, preferred_element_type=jnp.float32

time: 123 us -> 108 us (0.88)
  Pallas kernels: 81.2 us -> 65.5 us
    pallas_call x1, Pallas kernels: 28 us -> 7.32 us  [swap(): pl.pallas_call(functools.partial(swap_kernel, len(owns)), out_shape=[jax....]
    pallas_call x1, Pallas kernels: 53.2 us -> 58.2 us  [attention(): pl.pallas_call(functools.partial(attention_kernel, len(owns), width // lo...]
    unnamed x21 -> x19, local copies, waits for them, and re-layouts: 2.13 us -> 3.12 us
where the time goes in v2:
time: 108 us; the launch traced here: 107 us
  Pallas kernels  65.5 us (61%)
  matrix products  18.4 us (17%)
  local copies, waits for them, and re-layouts  11.4 us (11%)
  other arithmetic  10.5 us (10%)
  between operations  1.64 us (2%)
    pallas_call x1, Pallas kernels, attention(): pl.pallas_call(functools.partial(attention_kernel, len(owns), width // lo...  58.2 us
    pallas_call x1, Pallas kernels, swap(): pl.pallas_call(functools.partial(swap_kernel, len(owns)), out_shape=[jax....  7.32 us
    dot_general x1, matrix products, local(): jnp.dot(hidden, voc_down_flat, preferred_element_type=jnp.float32)  4.39 us
    dot_general x1, matrix products, local(): jnp.dot((magnitude * jnp.sin(phase_rows)).astype(jnp.bfloat16), sine_tabl...  4.32 us
    unnamed x19, local copies, waits for them, and re-layouts  3.12 us
    dot_general x1, matrix products, local(): jnp.dot((magnitude * jnp.cos(phase_rows)).astype(jnp.bfloat16), cosine_ta...  2.87 us
    dot_general x1, matrix products, local(): jnp.einsum('grc,gcd->rd', attended, attn_out_full, preferred_element_type...  2.54 us
    dot_general x1, matrix products, local(): jnp.einsum('gsc,gcd->sd', swapped[:, :window_rows], conv_out_full, prefer...  2.38 us

profile of v2, /device:TPU:0, one launch (start us, length us, event | category | flops | bytes accessed | tf_op | source)
XLA Modules:
  0.0 107.5 jit_solution(7581608471222627208)
XLA Ops:
  0.6 0.8 slice_bitcast_fusion.5
  1.4 0.7 broadcast_select_fusion
  2.3 0.7 pad.8.refs_2_
  3.7 1.9 %copy.30.refs_11_ = bf16[128,1282]{1,0:T(8,128)(2,1)} copy(bf16[128,1282]{0,1:T(8,128)(2,1)} %param.32) | data formatting | bytes 656384 | tf_op args[15]
  5.6 1.2 %reshape.195.refs_4_ = bf16[1,256]{1,0:T(2,128)(2,1)} reshape(bf16[256]{0:T(256)(128)(2,1)} %param.21) | data formatting | bytes 1024 | tf_op jit(solution)/shard_map/reshape | solution.py:522
  6.8 58.2 %shard_map.176 = (bf16[576,1024]{1,0:T(8,128)(2,1)}, bf16[4,576,128]{2,1,0:T(8,128)(2,1)}, bf16[4,128,1024]{2,1,0:T(8,128)(2,1)}, bf16[4,256,1024]{2,1,0:T(8,128...) custom-call(s32[1]{0:T(128)} %copy.49.refs_0_, ...), custom_call_target="tpu_custom_call" | custom-call | tf_op jit(solution)/shard_map/pallas_call | solution.py:492
  65.0 2.5 %bitcast_add_fusion = f32[576,1024]{1,0:T(8,128)S(1)} fusion(bf16[576,1024]{1,0:T(8,128)(2,1)} %get-tuple-element.14, bf16[4,576,128]{2,1,0:T(8,128)(2,1)} %get-tuple-element.15, bf16[4,128,1024]{2,1,0:T(8,128)(2,1)} %get-tuple-element.16), kind=kOutput, calls=%fused_computation.10 | convolution fusion | flops 605159424 | bytes 5177344 | tf_op jit(solution)/shard_map/grc,gcd->rd/dot_general | solution.py:648
  67.6 1.5 %slice.412 = f32[512,1024]{1,0:T(8,128)} slice(f32[576,1024]{1,0:T(8,128)S(1)} %bitcast_add_fusion), slice={[0:512], [0:1024]} | slice | bytes 4194304 | tf_op jit(solution)/shard_map/slice | solution.py:654
  69.1 2.0 %fusion.140 = (f32[552]{0:T(1024)S(1)}, f32[552,1024]{1,0:T(8,128)S(1)}) fusion(f32[20,1024]{1,0:T(8,128)S(1)} %get-tuple-element.33, f32[512,1024]{1,0:T(8,128)} %slice.412, f32[20,1024]{1,0:T(8,128)S(1)} %get-tuple-element.32, pred[552]{0:T(1024)(128)(4,1)S(1)} %fusion.102), kind=kLoop, calls=%fused_computation.217 | loop fusion | flops 2260440 | bytes 4524744 | tf_op jit(solution)/shard_map/reduce_sum | solution.py:15
  71.2 0.4 multiply_reduce_fusion
  71.6 0.3 multiply_convert_fusion
  71.8 0.9 copy-done.8
  72.8 0.5 fusion.32
  73.3 0.5 fusion.16
  73.8 0.2 copy-done.5
  74.1 2.3 %multiply_convert_fusion.2 = bf16[522,256]{1,0:T(8,128)(2,1)S(1)} fusion(bf16[552,256]{1,0:T(8,128)(2,1)S(1)} %fusion.16, f32[256]{0:T(256)S(1)} %bitcast.133, f32[256]{0:T(256)S(1)} %bitcast.134, f32[256]{0:T(256)S(1)} %bitcast.105, f32[256]{0:T(256)S(1)} %bitcast.106, f32[256]{0:T(256)S(1)} %bitcast.107, f32[256]{0:T(256)S(1)} %bitcast.108, ...), kind=kLoop, calls=%fused_computation.55 | loop fusion | flops 12962304 | bytes 8584192 | tf_op jit(solution)/shard_map/convert_element_type | solution.py:670
  76.4 0.8 fusion.70.refs_0_
  77.2 7.3 %shard_map.177 = bf16[4,144,256]{2,1,0:T(8,128)(2,1)} custom-call(bf16[4,144,256]{2,1,0:T(8,128)(2,1)} %fusion.70.refs_0_), custom_call_target="tpu_custom_call" | custom-call | tf_op jit(solution)/shard_map/pallas_call | solution.py:585
  84.5 2.4 %fusion.146 = (f32[138]{0:T(256)S(1)}, f32[138,1024]{1,0:T(8,128)S(1)}) fusion(bf16[4,256,1024]{2,1,0:T(8,128)(2,1)} %get-tuple-element.17, bf16[4,144,256]{2,1,0:T(8,128)(2,1)} %shard_map.177, f32[552,1024]{1,0:T(8,128)S(1)} %get-tuple-element.29, s32[]{:T(128)S(6)} %select_n.52), kind=kOutput, calls=%fused_computation.223 | convolution fusion | flops 289689472 | bytes 3523116 | tf_op jit(solution)/shard_map/gsc,gcd->sd/dot_general | solution.py:684
  87.3 0.4 fusion.147
  88.2 0.3 fusion.138
  88.8 4.4 %fusion.148 = (f32[132]{0:T(256)S(1)}, f32[132,512]{1,0:T(8,128)S(1)}) fusion(bf16[1536,512]{1,0:T(8,128)(2,1)} %bitcast.137, bf16[512,1536]{1,0:T(8,128)(2,1)} %bitcast.136, f32[132,512]{1,0:T(8,128)S(1)} %get-tuple-element.27, f32[132]{0:T(256)S(1)} %add_rsqrt_fusion.2, f32[132]{0:T(256)S(1)} %broadcast_multiply_fusion.3, ...), kind=kOutput, calls=%fused_computation.225 | convolution fusion | flops 428752768 | bytes 3958320 | tf_op jit(solution)/shard_map/dot_general | solution.py:703
  93.4 0.4 convolution_add_fusion.1
  93.9 1.1 %sine_multiply_fusion = (f32[41,1280]{1,0:T(8,128)S(1)}, f32[41,1280]{1,0:T(8,128)S(1)}) fusion(f32[1280]{0:T(1024)S(1)} %multiply_subtract_fusion.1, s32[41]{0:T(128)S(1)} %iota_multiply_fusion), kind=kLoop, calls=%fused_computation.121 | loop fusion | flops 577280 | bytes 425124 | tf_op jit(solution)/shard_map/mul | solution.py:42
  95.0 0.3 fusion.97
  95.3 0.7 multiply_add_fusion
  96.1 2.9 %fusion.4 = f32[132,1280]{1,0:T(8,128)} fusion(f32[656,1280]{1,0:T(8,128)S(1)} %bitcast.88, f32[641]{0:T(1024)S(1)} %bitcast.92, f32[132,1282]{1,0:T(8,128)S(1)} %convolution_add_fusion.1), kind=kOutput, calls=%fused_computation.14 | convolution fusion | flops 218501520 | bytes 4833280 | tf_op jit(solution)/shard_map/dot_general | solution.py:717
  99.0 4.3 %fusion.3 = f32[132,1280]{1,0:T(8,128)} fusion(f32[132,1280]{1,0:T(8,128)} %fusion.4, f32[656,1280]{1,0:T(8,128)S(1)} %bitcast.89, f32[641]{0:T(1024)S(1)} %bitcast.93, pred[641]{0:T(1024)(128)(4,1)S(1)} %bitcast.135, f32[132]{0:T(256)S(1)} %and_convert_fusion, f32[132,1282]{1,0:T(8,128)} %copy-done), kind=kOutput, calls=%fused_computation.8 | convolution fusion | flops 219659920 | bytes 5531648 | tf_op jit(solution)/shard_map/dot_general | solution.py:719
  103.3 1.7 %reshape.200 = f32[132,4,320]{2,1,0:T(4,128)S(1)} reshape(f32[132,1280]{1,0:T(8,128)} %fusion.3) | data formatting | bytes 1351680 | tf_op jit(solution)/shard_map/reshape | solution.py:724
  105.0 0.6 fusion.142
  105.9 0.8 div.66
  106.7 0.8 slice.449
  (51 shorter events, 1.9 us)
Async XLA Ops:
  71.5 1.2 %copy-start.8 = (bf16[2,1024,256]{2,1,0:T(8,128)(2,1)S(1)}, bf16[2,1024,256]{2,1,0:T(8,128)(2,1)}, u32[]{:S(2)}) copy-start(bf16[2,1024,256]{2,1,0:T(8,128)(2,1)} %param.25) | copy-start | bytes 3145732
  73.3 0.8 copy-start.5
  84.5 2.8 %copy-start.4 = (bf16[4,256,512]{2,1,0:T(8,128)(2,1)S(1)}, bf16[4,256,512]{2,1,0:T(8,128)(2,1)}, u32[]{:S(2)}) copy-start(bf16[4,256,512]{2,1,0:T(8,128)(2,1)} %get-tuple-element.18) | copy-start | bytes 3145732
  86.9 1.2 %copy-start.6 = (f32[7,512]{1,0:T(8,128)S(1)}, f32[7,512]{1,0:T(8,128)}, u32[]{:S(2)}) copy-start(f32[7,512]{1,0:T(8,128)} %param.29) | copy-start | bytes 43012
  87.3 0.7 copy-start.1
  88.7 4.6 %copy-start.3 = (bf16[4,128,1282]{2,1,0:T(8,128)(2,1)S(1)}, bf16[4,128,1282]{2,1,0:T(8,128)(2,1)}, u32[]{:S(2)}) copy-start(bf16[4,128,1282]{2,1,0:T(8,128)(2,1)} %get-tuple-element.21) | copy-start | bytes 3938308
  88.7 4.6 %copy-start.7 = (f32[1282]{0:T(1024)S(1)}, f32[1282]{0:T(1024)}, u32[]{:S(2)}) copy-start(f32[1282]{0:T(1024)} %param.33) | copy-start | bytes 15388
  93.8 2.3 %copy-start = (f32[132,1282]{1,0:T(8,128)}, f32[132,1282]{1,0:T(8,128)S(1)}, u32[]{:S(2)}) copy-start(f32[132,1282]{1,0:T(8,128)S(1)} %convolution_add_fusion.1) | copy-start | bytes 2030692
  105.0 1.7 %copy-start.2 = (bf16[138,1024]{1,0:T(8,128)(2,1)S(1)}, bf16[138,1024]{1,0:T(8,128)(2,1)}, u32[]{:S(2)}) copy-start(bf16[138,1024]{1,0:T(8,128)(2,1)} %copy-done.1) | copy-start | bytes 847876

commit v3 on v2

--- a/solution.py
+++ b/solution.py
@@ -28,27 +28,33 @@
     return result
 
 
-def synthesis_tables(bin_count, fft_size, window):
+def synthesis_tables(bin_count, fft_size, parts, window):
     fine = 16
     coarse = -(-bin_count // fine)
+    hop = fft_size // parts
     unit = 2.0 * math.pi / fft_size
-    samples = lax.broadcasted_iota(jnp.int32, (coarse, fft_size), 1)
-    steps = lax.broadcasted_iota(jnp.int32, (coarse, fft_size), 0) * fine
-    big = unit * (steps * samples % fft_size).astype(jnp.float32)
-    samples = lax.broadcasted_iota(jnp.int32, (fine, fft_size), 1)
-    steps = lax.broadcasted_iota(jnp.int32, (fine, fft_size), 0)
-    small = unit * (steps * samples % fft_size).astype(jnp.float32)
+
+    def angles(count, stride):
+        shape = (parts, count, hop)
+        samples = lax.broadcasted_iota(jnp.int32, shape, 0) * hop + lax.broadcasted_iota(
+            jnp.int32, shape, 2
+        )
+        steps = lax.broadcasted_iota(jnp.int32, shape, 1) * stride
+        return unit * (steps * samples % fft_size).astype(jnp.float32)
+
+    big, small = angles(coarse, fine), angles(fine, 1)
+    window = window.reshape(parts, 1, hop)
     big_cos, big_sin, small_cos, small_sin = lax.optimization_barrier(
         (jnp.cos(big) * window, jnp.sin(big) * window, jnp.cos(small), jnp.sin(small))
     )
-    cosine = big_cos[:, None] * small_cos[None] - big_sin[:, None] * small_sin[None]
-    sine = big_sin[:, None] * small_cos[None] + big_cos[:, None] * small_sin[None]
-    bins = lax.broadcasted_iota(jnp.int32, (coarse * fine, 1), 0)
+    cosine = big_cos[:, :, None] * small_cos[:, None] - big_sin[:, :, None] * small_sin[:, None]
+    sine = big_sin[:, :, None] * small_cos[:, None] + big_cos[:, :, None] * small_sin[:, None]
+    bins = lax.broadcasted_iota(jnp.int32, (1, coarse * fine, 1), 1)
     edge = (bins == 0) | (bins == bin_count - 1)
     factor = jnp.where(edge, 1.0, 2.0) / fft_size
-    cosine = factor * cosine.reshape(coarse * fine, fft_size)
-    sine = jnp.where(edge, 0.0, -factor * sine.reshape(coarse * fine, fft_size))
-    return cosine[:bin_count].astype(jnp.bfloat16), sine[:bin_count].astype(jnp.bfloat16)
+    cosine = factor * cosine.reshape(parts, coarse * fine, hop)
+    sine = jnp.where(edge, 0.0, -factor * sine.reshape(parts, coarse * fine, hop))
+    return cosine[:, :bin_count].astype(jnp.bfloat16), sine[:, :bin_count].astype(jnp.bfloat16)
 
 
 MESH = pl.DeviceIdType.MESH
@@ -334,6 +340,11 @@
         view = kvbuf.at[block, piece]
         return remote(view, view, l_send.at[step, piece], l_recv.at[step, piece], seq=at.seq - 1)
 
+    segments = (
+        (0, rows, HALO),
+        (rows, rows + HALO, -rows),
+        (rows + HALO, total, 0),
+    )
     own_kv = kvbuf.at[at.seq]
     for index, spread in enumerate(spreads):
         spread.relay()
@@ -345,7 +356,10 @@
             whole = jnp.concatenate(
                 [emb[block, pl.ds(offset, size)] for block in range(blocks)], axis=1
             )
-            emb_out[pl.ds(offset, size)] = whole
+            for begin_at, stop_at, shift in segments:
+                low, high = max(offset, begin_at), min(offset + size, stop_at)
+                if low < high:
+                    emb_out[pl.ds(low + shift, high - low)] = whole[low - offset : high - offset]
             normed = norm_rows(whole.astype(jnp.float32)).astype(jnp.bfloat16)
             query = unit(jnp.dot(normed, attn_ref[0], preferred_element_type=jnp.float32))
             for h in range(local_heads):
@@ -471,7 +485,9 @@
     lax.fori_loop(0, at.seqs - 1, drain, 0)
     gather.finish()
     for block in range(blocks):
-        att_out[block] = att[block]
+        for begin_at, stop_at, shift in segments:
+            span = pl.ds(begin_at + shift, stop_at - begin_at)
+            att_out[block, span] = att[block, pl.ds(begin_at, stop_at - begin_at)]
     for weight in weights:
         weight.finish()
 
@@ -648,29 +664,23 @@
     stream_rows = embedded.astype(jnp.float32) + jnp.einsum(
         "grc,gcd->rd", attended, attn_out_full, preferred_element_type=jnp.float32
     )
-    stream_rims = jnp.concatenate(
-        [
-            stream_rows[frame_count + HALO - conv_reach : frame_count + HALO],
-            stream_rows[:frame_count],
-            stream_rows[frame_count + HALO : frame_count + HALO + conv_reach],
-        ]
-    )
-    rim_ids = seq_index * frame_count - conv_reach + lax.broadcasted_iota(
-        jnp.int32, (frame_count + 2 * conv_reach, 1), 0
-    )
-    stream_rims = jnp.where((rim_ids >= 0) & (rim_ids < total_frames), stream_rims, 0.0)
+    rim_ids = seq_index * frame_count - HALO + lax.broadcasted_iota(
+        jnp.int32, (frame_count + 2 * HALO, 1), 0
+    )
+    stream_rims = jnp.where((rim_ids >= 0) & (rim_ids < total_frames), stream_rows, 0.0)
     conv_normed = layer_norm(stream_rims).astype(jnp.bfloat16)
     residual_window = lax.dynamic_slice_in_dim(
-        stream_rims, group_index * slab_rows + conv_reach - vocoder_rim, window_rows, 0
+        stream_rims, group_index * slab_rows + HALO - vocoder_rim, window_rows, 0
     )
     gate_value = jnp.dot(conv_normed, conv_in[0], preferred_element_type=jnp.float32)
     gate_signal = jnp.dot(conv_normed, conv_in[1], preferred_element_type=jnp.float32)
     gated_rows = (gate_value * jax.nn.sigmoid(gate_signal)).astype(jnp.bfloat16)
     depth_rows = depthwise(conv_kernel, gated_rows)
     activated = (depth_rows * jax.nn.sigmoid(depth_rows)).astype(jnp.bfloat16)
+    first = HALO - conv_reach
     windows = jnp.stack(
         [
-            activated[member * slab_rows : member * slab_rows + window_rows]
+            activated[first + member * slab_rows : first + member * slab_rows + window_rows]
             for member in range(group_count)
         ]
     )
@@ -708,26 +718,27 @@
     bin_count = spectrum.shape[1] // 2
     magnitude = jnp.minimum(jnp.exp(spectrum[:, :bin_count]), 100.0)
     phase_rows = spectrum[:, bin_count:]
-    coefficients = jnp.concatenate(
-        [magnitude * jnp.cos(phase_rows), magnitude * jnp.sin(phase_rows)], axis=1
-    )
     sample_ids = lax.broadcasted_iota(jnp.int32, (fft_size,), 0).astype(jnp.float32)
     hann_window = 0.5 - 0.5 * jnp.cos(2.0 * math.pi / fft_size * sample_ids)
-    cosine_table, sine_table = synthesis_tables(bin_count, fft_size, hann_window)
-    wave_rows = jnp.dot(
-        (magnitude * jnp.cos(phase_rows)).astype(jnp.bfloat16), cosine_table, preferred_element_type=jnp.float32
-    ) + jnp.dot(
-        (magnitude * jnp.sin(phase_rows)).astype(jnp.bfloat16), sine_table, preferred_element_type=jnp.float32
-    )
+    cosine_table, sine_table = synthesis_tables(bin_count, fft_size, intersection, hann_window)
     wave_ids = first_frame + half_voc + lax.broadcasted_iota(jnp.int32, (voc_rows, 1), 0)
-    exists = ((wave_ids >= 0) & (wave_ids < total_frames)).astype(jnp.float32)
-    framed = (wave_rows * exists).reshape(voc_rows, intersection, HOP)
-    env_rows = (exists * (hann_window * hann_window)[None, :]).reshape(voc_rows, intersection, HOP)
+    exists = (wave_ids >= 0) & (wave_ids < total_frames)
+    magnitude = jnp.where(exists, magnitude, 0.0)
+    real_rows = (magnitude * jnp.cos(phase_rows)).astype(jnp.bfloat16)
+    imag_rows = (magnitude * jnp.sin(phase_rows)).astype(jnp.bfloat16)
+    env_rows = (exists.astype(jnp.float32) * (hann_window * hann_window)[None, :]).reshape(
+        voc_rows, intersection, HOP
+    )
     audio_sum = jnp.zeros((slab_rows, HOP), jnp.float32)
     energy = jnp.zeros((slab_rows, HOP), jnp.float32)
     for quarter in range(intersection):
         begin = intersection - quarter
-        audio_sum = audio_sum + framed[begin : begin + slab_rows, quarter]
+        for part_rows, table in ((real_rows, cosine_table), (imag_rows, sine_table)):
+            audio_sum = audio_sum + jnp.dot(
+                part_rows[begin : begin + slab_rows],
+                table[quarter],
+                preferred_element_type=jnp.float32,
+            )
         energy = energy + env_rows[begin : begin + slab_rows, quarter]
     waveform = (audio_sum / energy).reshape(slab_rows * HOP)
     return (feature_out, waveform)

time: 108 us -> 101 us (0.935)
  matrix products: 18.4 us -> 14.3 us
  local copies, waits for them, and re-layouts: 11.4 us -> 7.79 us
  other arithmetic: 10.5 us -> 11.8 us
    dot_general x2 -> x8, matrix products: 7.19 us -> 3.06 us  [local(): jnp.dot(part_rows[begin:begin + slab_rows], table[quarter], preferred_ele...]
    slice x3 -> x0, local copies, waits for them, and re-layouts: 2.1 us -> none  [the longest x1 1.53 us: local(): stream_rows[:frame_count]]
    reduce_sum x2 -> x1, other arithmetic: 2.37 us -> 0.32 us  [layer_norm(): average = jnp.mean(values, axis=-1, keepdims=True)]
    convert_element_type x1, other arithmetic: 0.01 us -> 1.61 us  [local(): imag_rows = (magnitude * jnp.sin(phase_rows)).astype(jnp.bfloat16)]
    another operation x1 -> x2, other arithmetic: 0.75 us -> 1.9 us  [local(): jnp.stack([activated[member * slab_rows:member * slab_rows + window_rows]...]
    unnamed x19 -> x13, local copies, waits for them, and re-layouts: 3.12 us -> 3.08 us
where the time goes in v3:
time: 101 us
  Pallas kernels  65.4 us (65%)
  matrix products  14.3 us (14%)
  other arithmetic  11.8 us (12%)
  local copies, waits for them, and re-layouts  7.79 us (8%)
  between operations  1.68 us (2%)
    pallas_call x1, Pallas kernels, attention(): pl.pallas_call(functools.partial(attention_kernel, len(owns), width // lo...  58.1 us
    pallas_call x1, Pallas kernels, swap(): pl.pallas_call(functools.partial(swap_kernel, len(owns)), out_shape=[jax....  7.34 us
    dot_general x1, matrix products, local(): jnp.dot(hidden, voc_down_flat, preferred_element_type=jnp.float32)  4.39 us
    unnamed x13, local copies, waits for them, and re-layouts  3.08 us
    dot_general x8, matrix products, local(): jnp.dot(part_rows[begin:begin + slab_rows], table[quarter], preferred_ele...  3.06 us
    dot_general x1, matrix products, local(): jnp.einsum('grc,gcd->rd', attended, attn_out_full, preferred_element_type...  2.68 us
    convert_element_type x1, other arithmetic, local(): activated = (depth_rows * jax.nn.sigmoid(depth_rows)).astype(jnp.bfloat16)  2.44 us
    dot_general x1, matrix products, local(): jnp.einsum('gsc,gcd->sd', swapped[:, :window_rows], conv_out_full, prefer...  2.38 us

profile of v3, /device:TPU:0, one launch (start us, length us, event | category | flops | bytes accessed | tf_op | source)
XLA Modules:
  0.0 101.0 jit_solution(11161274389610927602)
XLA Ops:
  0.6 0.8 slice_bitcast_fusion.21
  1.4 0.7 broadcast_select_fusion
  2.3 0.7 pad.8.refs_2_
  3.7 1.9 %copy.27.refs_11_ = bf16[128,1282]{1,0:T(8,128)(2,1)} copy(bf16[128,1282]{0,1:T(8,128)(2,1)} %param.32) | data formatting | bytes 656384 | tf_op args[15]
  5.6 1.2 %reshape.194.refs_4_ = bf16[1,256]{1,0:T(2,128)(2,1)} reshape(bf16[256]{0:T(256)(128)(2,1)} %param.21) | data formatting | bytes 1024 | tf_op jit(solution)/shard_map/reshape | solution.py:538
  6.8 58.1 %shard_map.176 = (bf16[576,1024]{1,0:T(8,128)(2,1)}, bf16[4,576,128]{2,1,0:T(8,128)(2,1)}, bf16[4,128,1024]{2,1,0:T(8,128)(2,1)}, bf16[4,256,1024]{2,1,0:T(8,128...) custom-call(s32[1]{0:T(128)} %copy.29.refs_0_, ...), custom_call_target="tpu_custom_call" | custom-call | tf_op jit(solution)/shard_map/pallas_call | solution.py:508
  64.9 2.7 %fusion.144 = (f32[576]{0:T(1024)S(1)}, f32[576,1024]{1,0:T(8,128)S(1)}) fusion(bf16[4,576,128]{2,1,0:T(8,128)(2,1)} %get-tuple-element.15, bf16[4,128,1024]{2,1,0:T(8,128)(2,1)} %get-tuple-element.16, bf16[576,1024]{1,0:T(8,128)(2,1)} %get-tuple-element.14, pred[576]{0:T(1024)(128)(4,1)S(1)} %fusion.104), kind=kOutput, calls=%fused_computation.233 | convolution fusion | flops 606338496 | bytes 5180224 | tf_op jit(solution)/shard_map/grc,gcd->rd/dot_general | solution.py:664
  67.6 0.4 multiply_reduce_fusion
  68.3 0.9 copy-done.5
  69.2 0.5 fusion.26
  69.7 0.5 fusion.9
  70.5 2.4 %multiply_convert_fusion.2 = bf16[546,256]{1,0:T(8,128)(2,1)S(1)} fusion(bf16[576,256]{1,0:T(8,128)(2,1)S(1)} %fusion.9, f32[256]{0:T(256)S(1)} %bitcast.162, f32[256]{0:T(256)S(1)} %bitcast.163, f32[256]{0:T(256)S(1)} %bitcast.134, f32[256]{0:T(256)S(1)} %bitcast.135, f32[256]{0:T(256)S(1)} %bitcast.136, f32[256]{0:T(256)S(1)} %bitcast.137, ...), kind=kLoop, calls=%fused_computation.57 | loop fusion | flops 13558272 | bytes 8977408 | tf_op jit(solution)/shard_map/convert_element_type | solution.py:679
  73.0 0.7 fusion.68.refs_0_
  73.8 7.3 %shard_map.177 = bf16[4,144,256]{2,1,0:T(8,128)(2,1)} custom-call(bf16[4,144,256]{2,1,0:T(8,128)(2,1)} %fusion.68.refs_0_), custom_call_target="tpu_custom_call" | custom-call | tf_op jit(solution)/shard_map/pallas_call | solution.py:601
  81.1 2.4 %fusion.145 = (f32[138]{0:T(256)S(1)}, f32[138,1024]{1,0:T(8,128)S(1)}) fusion(bf16[4,256,1024]{2,1,0:T(8,128)(2,1)} %get-tuple-element.17, bf16[4,144,256]{2,1,0:T(8,128)(2,1)} %shard_map.177, f32[576,1024]{1,0:T(8,128)S(1)} %get-tuple-element.84, s32[]{:T(128)S(6)} %select_n.56), kind=kOutput, calls=%fused_computation.234 | convolution fusion | flops 289689472 | bytes 3523116 | tf_op jit(solution)/shard_map/gsc,gcd->sd/dot_general | solution.py:694
  83.9 0.4 fusion.146
  85.3 4.4 %fusion.147 = (f32[132]{0:T(256)S(1)}, f32[132,512]{1,0:T(8,128)S(1)}) fusion(bf16[1536,512]{1,0:T(8,128)(2,1)} %bitcast.165, bf16[512,1536]{1,0:T(8,128)(2,1)} %bitcast.164, f32[132,512]{1,0:T(8,128)S(1)} %get-tuple-element.27, f32[132]{0:T(256)S(1)} %add_rsqrt_fusion.2, f32[132]{0:T(256)S(1)} %broadcast_multiply_fusion.3, ...), kind=kOutput, calls=%fused_computation.236 | convolution fusion | flops 428752768 | bytes 3958320 | tf_op jit(solution)/shard_map/dot_general | solution.py:713
  89.9 0.4 convolution_add_fusion
  90.4 1.6 %multiply_convert_fusion.3 = (bf16[132,641]{1,0:T(8,128)(2,1)S(1)}, bf16[132,641]{1,0:T(8,128)(2,1)S(1)}) fusion(f32[132,1282]{1,0:T(8,128)S(1)} %convolution_add_fusion, pred[132]{0:T(512)(128)(4,1)S(1)} %get-tuple-element.93), kind=kLoop, calls=%fused_computation.76 | loop fusion | flops 507672 | bytes 1015476 | tf_op jit(solution)/shard_map/convert_element_type | solution.py:728
  92.1 1.3 %sine_multiply_fusion = (f32[4,41,320]{2,1,0:T(8,128)S(1)}, f32[4,41,320]{2,1,0:T(8,128)S(1)}) fusion(f32[4,320]{1,0:T(4,128)S(1)} %multiply_subtract_fusion.1, s32[4]{0:T(128)S(1)} %iota_multiply_fusion, s32[41]{0:T(128)S(1)} %iota_multiply_fusion.1), kind=kLoop, calls=%fused_computation.113 | loop fusion | flops 629760 | bytes 425140 | tf_op jit(solution)/shard_map/mul | solution.py:48
  93.4 0.5 fusion.99
  93.9 0.8 multiply_add_fusion
  94.8 1.2 %fusion.1 = (bf16[4,656,320]{2,1,0:T(8,128)(2,1)S(1)}, bf16[4,656,320]{2,1,0:T(8,128)(2,1)S(1)}) fusion(f32[4,41,16,320]{3,2,1,0:T(8,128)S(1)} %get-tuple-element.30, f32[656]{0:T(1024)S(1)} %fusion.107, pred[656]{0:T(1024)(128)(4,1)S(1)} %fusion.105, f32[4,41,16,320]{3,2,1,0:T(8,128)S(1)} %get-tuple-element.31, f32[656]{0:T(1024)S(1)} %select_multiply_fusion), kind=kLoop, calls=%fused_computation.2 | loop fusion | flops 4198400 | bytes 10082064 | tf_op jit(solution)/shard_map/convert.1
  96.3 0.4 convolution_add_fusion.8
  96.7 0.4 convolution_add_fusion.7
  97.1 0.4 convolution_add_fusion.6
  97.4 0.4 convolution_add_fusion.5
  97.8 0.4 convolution_add_fusion.4
  98.2 0.4 convolution_add_fusion.3
  98.9 0.4 fusion.10
  99.5 0.8 reshape.199
  100.3 0.8 slice.484
  (49 shorter events, 3.2 us)
Async XLA Ops:
  68.0 1.2 %copy-start.5 = (bf16[2,1024,256]{2,1,0:T(8,128)(2,1)S(1)}, bf16[2,1024,256]{2,1,0:T(8,128)(2,1)}, u32[]{:S(2)}) copy-start(bf16[2,1024,256]{2,1,0:T(8,128)(2,1)} %param.25) | copy-start | bytes 3145732
  69.7 0.8 copy-start.2
  81.1 2.8 %copy-start.1 = (bf16[4,256,512]{2,1,0:T(8,128)(2,1)S(1)}, bf16[4,256,512]{2,1,0:T(8,128)(2,1)}, u32[]{:S(2)}) copy-start(bf16[4,256,512]{2,1,0:T(8,128)(2,1)} %get-tuple-element.18) | copy-start | bytes 3145732
  83.5 1.2 %copy-start.3 = (f32[7,512]{1,0:T(8,128)S(1)}, f32[7,512]{1,0:T(8,128)}, u32[]{:S(2)}) copy-start(f32[7,512]{1,0:T(8,128)} %param.29) | copy-start | bytes 43012
  85.3 4.6 %copy-start = (bf16[4,128,1282]{2,1,0:T(8,128)(2,1)S(1)}, bf16[4,128,1282]{2,1,0:T(8,128)(2,1)}, u32[]{:S(2)}) copy-start(bf16[4,128,1282]{2,1,0:T(8,128)(2,1)} %get-tuple-element.21) | copy-start | bytes 3938308
  85.3 4.6 %copy-start.4 = (f32[1282]{0:T(1024)S(1)}, f32[1282]{0:T(1024)}, u32[]{:S(2)}) copy-start(f32[1282]{0:T(1024)} %param.33) | copy-start | bytes 15388
